TPU v7x, 32 devices: a whole 2x2x4 slice. The times are simulated.
32 devices in a mesh: dp: 4 (over y, core), fsdp: 8 (over z, x).
Axes of the slice: x: 2, y: 2, z: 4, core: 2. Of those that a mesh axis runs over, the one named last changes fastest.
Arguments:
- latents: int32 [256, 64, 32], P(('dp', 'fsdp')), may hold values from 0 to 31
- actions: int32 [256, 64], P(('dp', 'fsdp')), may hold values from 0 to 17, as said below
- game_ids: int32 [256], P(('dp', 'fsdp')), may hold values from 0 to 25
- action_masks: int32 [26, 18], replicated, may hold values from 0 to 1, as said below
- valid_steps: int32 [256, 64], P(('dp', 'fsdp')), may hold values from 0 to 1, as said below
- target_bins: int32 [256, 64, 2], P(('dp', 'fsdp')), may hold values from 0 to 253
- target_fracs: float32 [256, 64, 2], P(('dp', 'fsdp')), may hold values from 0 to 1
- continues: int32 [256, 64], P(('dp', 'fsdp')), may hold values 0 or 1
- owner_order: int32 [192], replicated, may hold values from 0 to 191, each once
- blocks: float32 [192, 128, 128], P('fsdp'), may hold values from -0.25 to 0.25
- block_first: float32 [192, 128, 128], P('fsdp'), may hold values from -1.5258789e-05 to 1.5258789e-05
- block_second: float32 [192, 128, 128], P('fsdp'), may hold values from 5.649883e-12 to 2.2554868e-11
- left_stat: float32 [192, 128, 128], P('fsdp'), may hold values from -2.85843873e-09 to 2.9156075e-09, as said below
- right_stat: float32 [192, 128, 128], P('fsdp'), may hold values from -2.85843873e-09 to 2.9156075e-09, as said below
- left_basis: float32 [192, 128, 128], P('fsdp'), may hold values from -1 to 1, as said below
- right_basis: float32 [192, 128, 128], P('fsdp'), may hold values from -1 to 1, as said below
- latent_maps: float32 [2048, 512], P('fsdp'), may hold values from -0.625 to 0.625
- latent_first: float32 [2048, 512], P('fsdp'), may hold values from -1.5258789e-05 to 1.5258789e-05
- latent_second: float32 [2048, 512], P('fsdp'), may hold values from 5.649883e-12 to 2.2554868e-11
- head_weights: float32 [513, 529], replicated, may hold values from -0.625 to 0.625
- head_first: float32 [513, 529], replicated, may hold values from -1.5258789e-05 to 1.5258789e-05
- head_second: float32 [513, 529], replicated, may hold values from 5.649883e-12 to 2.2554868e-11
- small_params: float32 [24, 512], replicated
- small_first: float32 [24, 512], replicated, may hold values from -1.5258789e-05 to 1.5258789e-05
- small_second: float32 [24, 512], replicated, may hold values from 5.649883e-12 to 2.2554868e-11
- ema_critic: float32 [513, 255], replicated, may hold values from -0.15625 to 0.15625
Outputs:
- loss: float32 [], replicated
- grad_norm: float32 [], replicated
- blocks_new: float32 [192, 128, 128], P('fsdp')
- block_first_new: float32 [192, 128, 128], P('fsdp')
- block_second_new: float32 [192, 128, 128], P('fsdp')
- left_stat_new: float32 [192, 128, 128], P('fsdp')
- right_stat_new: float32 [192, 128, 128], P('fsdp')
- left_basis_new: float32 [192, 128, 128], P('fsdp')
- right_basis_new: float32 [192, 128, 128], P('fsdp')
- latent_maps_new: float32 [2048, 512], P('fsdp')
- latent_first_new: float32 [2048, 512], P('fsdp')
- latent_second_new: float32 [2048, 512], P('fsdp')
- head_weights_new: float32 [513, 529], replicated
- head_first_new: float32 [513, 529], replicated
- head_second_new: float32 [513, 529], replicated
- small_params_new: float32 [24, 512], replicated
- small_first_new: float32 [24, 512], replicated
- small_second_new: float32 [24, 512], replicated
- ema_critic_new: float32 [513, 255], replicated
Inputs may be any that keep to these rules, and one draw needn't show every extreme that they name: `actions`: every action is legal in its sequence's game. `action_masks`: every game allows action 0. `valid_steps`: each sequence is 1 on a prefix of 16 frames or more and 0 after it. `owner_order`: a permutation of the blocks. `left_stat`: symmetric positive definite. `right_stat`: symmetric positive definite. `left_basis`: orthogonal. `right_basis`: orthogonal.
All inputs are finite; a program needn't handle non-finite values. Where the computation divides by a largest or mean magnitude, that divisor is 1e-20 or more. No bound on the sum of `continues` on one device may be relied on, other than what follows from the above.
Results may differ from a plain program's by a relative error of at most 0.0053.
Values may be sent and summed in bfloat16 or wider, within the bound.
No kernel may reach another device: no remote copies, remote signals or barrier semaphores. Data moves between devices by JAX's collectives and lax.ppermute only.
A program may use at most 192 MiB of HBM per device.

v0:
```python
import functools
import math

import jax
import jax.numpy as jnp
from jax import lax
from jax.experimental import pallas as pl
from jax.experimental.pallas import tpu as pltpu
from jax.sharding import PartitionSpec as P

D = 512
NH = 8
DH = 64
FF = 2048
GROUPS = 32
CLASSES = 32
LAT = 1024
BINS = 255
NA = 18
LAYERS = 1
F = 64
NGAME = 26
BS = 128
STEP = 10
PAN = 16
PACK = 8
HEAD_COLS = 640
PACK_ROWS = 3072
MAP_CHUNKS = ((0, 1), (2,), (3,))
PART_ROWS = (384, 368, 368)
TM = 256
GELU_A = math.sqrt(2.0 / math.pi)
GELU_B = 0.044715


HIGHEST = lax.Precision.HIGHEST
beta_one = 0.9
beta_two = 0.99
epsilon = 1e-08
learn_rate = 0.03
small_rate = 0.15
weight_decay = 0.01
clip_norm = 0.05
ema_rate = 0.98
norm_eps = 1e-05


def positions(frames, width):
    frame_index = jnp.arange(frames).astype(jnp.float32)[:, None]
    feature = jnp.arange(width)
    freq = jnp.exp(-(feature // 2 * 2).astype(jnp.float32) * (math.log(10000.0) / width))
    angle = frame_index * freq[None, :]
    return jnp.where(feature % 2 == 0, jnp.sin(angle), jnp.cos(angle))


def halves(size):
    return [1 << bit for bit in reversed(range(size.bit_length() - 1))]


def swap(value, axis, size, bit):
    return lax.ppermute(value, axis, [(i, i ^ bit) for i in range(size)])


def sum_small(value, dp, fsdp):
    for axis, size in (("dp", dp), ("fsdp", fsdp)):
        for bit in reversed(halves(size)):
            value = value + swap(value, axis, size, bit)
    return value


def part_orders(dp, fsdp):
    core, tall = [("dp", dp, bit) for bit in reversed(halves(dp))]
    deep, near, side = [("fsdp", fsdp, bit) for bit in halves(fsdp)]
    return (
        (core, tall, side, near, deep),
        (core, side, near, deep, tall),
        (core, near, tall, side, deep),
    )


def order_index(order, dp_here, fsdp_here):
    dp_index = jnp.zeros((), jnp.int32)
    fsdp_index = jnp.zeros((), jnp.int32)
    spot = jnp.arange(1 << len(order))
    for place, (axis, _, bit) in enumerate(order):
        flag = (spot >> (len(order) - 1 - place)) & 1
        if axis == "dp":
            dp_index = dp_index + flag * bit
        else:
            fsdp_index = fsdp_index + flag * bit
    return dp_index ^ dp_here, fsdp_index ^ fsdp_here


def scatter_sum(held, sent, order, wide_stages):
    for place, (axis, size, bit) in enumerate(order):
        got = swap(sent, axis, size, bit)
        held = held + got.astype(jnp.float32)
        half = held.shape[0] // 2
        if half:
            held, sent = held[:half], held[half:]
            if place + 1 < len(order) - wide_stages:
                sent = sent.astype(jnp.bfloat16)
    return held[0]


def gather_doubling(value, order):
    held = value[None]
    for axis, size, bit in reversed(order):
        held = jnp.concatenate([held, swap(held, axis, size, bit)], 0)
    return held


def inverse_place(order, dp, fsdp, dp_here, fsdp_here):
    dp_id = jnp.arange(dp)[None, :] ^ dp_here
    fsdp_id = jnp.arange(fsdp)[:, None] ^ fsdp_here
    spot = jnp.zeros((fsdp, dp), jnp.int32)
    for place, (axis, _, bit) in enumerate(order):
        source = dp_id if axis == "dp" else fsdp_id
        flag = (source & bit) // bit
        spot = spot + flag * (1 << (len(order) - 1 - place))
    return spot


def placed_units(dp, fsdp):
    dp_here = lax.axis_index("dp")
    fsdp_here = lax.axis_index("fsdp")
    units = []
    spots = []
    for order in part_orders(dp, fsdp):
        dp_index, fsdp_index = order_index(order, dp_here, fsdp_here)
        units.append(fsdp_index * dp + dp_index)
        spots.append(inverse_place(order, dp, fsdp, dp_here, fsdp_here).reshape(-1))
    return jnp.stack(units), jnp.stack(spots)


def gathered_pieces(blocks_low, maps_low, dp, fsdp):
    dp_here = lax.axis_index("dp")
    quarter = blocks_low.shape[0] // dp
    piece_rows = maps_low.shape[0] // dp
    own_blocks = lax.dynamic_slice_in_dim(blocks_low, dp_here * quarter, quarter, 0)
    own_maps = lax.dynamic_slice_in_dim(maps_low, dp_here * piece_rows, piece_rows, 0)
    pieces = []
    for part, order in enumerate(part_orders(dp, fsdp)):
        piece = jnp.concatenate(
            [own_blocks[2 * part], own_blocks[2 * part + 1]]
            + [own_maps[:, c * BS : (c + 1) * BS] for c in MAP_CHUNKS[part]],
            0,
        )
        held = gather_doubling(piece, order[2:])
        both = [held, swap(held, *order[1])]
        pieces += both + [swap(piece, *order[0]) for piece in both]
    return pieces


def reduced_grads(outs, sums, slots, map_rows, dp, fsdp):
    if (dp, fsdp) != (4, 8):
        both = ("dp", "fsdp")
        block_grad = lax.psum(
            lax.psum_scatter(outs[0], "fsdp", scatter_dimension=0, tiled=True), "dp"
        )
        maps_grad = lax.psum(
            lax.psum_scatter(outs[1], "fsdp", scatter_dimension=0, tiled=True), "dp"
        )
        heads = lax.psum(outs[2], both)
        sums = lax.psum(sums, both)
        held = lax.psum(jnp.sum(block_grad * block_grad) + jnp.sum(maps_grad * maps_grad), "fsdp")
        return block_grad, maps_grad, heads, held + jnp.sum(heads * heads), sums
    dp_here = lax.axis_index("dp")
    fsdp_here = lax.axis_index("fsdp")
    parts = [
        scatter_sum(outs[2 * part], outs[2 * part + 1], order, 2)
        for part, order in enumerate(part_orders(dp, fsdp))
    ]
    cut = 2 * BS
    own_blocks = jnp.concatenate([part[:cut] for part in parts], 0)
    own_maps = jnp.concatenate([parts[0][cut:], parts[1][cut : cut + 64], parts[2][cut : cut + 64]], 0)
    own_heads = jnp.concatenate([parts[1][cut + 64 :], parts[2][cut + 64 :]], 0)
    own_square = sum(jnp.sum(part * part) for part in parts)
    sums = sum_small(jnp.concatenate([sums, own_square[None]]), dp, fsdp)
    dp_order = [("dp", dp, bit) for bit in reversed(halves(dp))]
    spot = inverse_place(dp_order, dp, 1, dp_here, 0).reshape(-1)
    shard = gather_doubling(jnp.concatenate([own_blocks, own_maps], 0), dp_order)
    shard = shard[spot]
    count = slots // dp * BS
    piece_rows = map_rows // dp
    block_grad = shard[:, :count].reshape(slots, BS, BS)
    maps_grad = (
        shard[:, count:]
        .reshape(dp, D // BS, piece_rows, BS)
        .transpose(0, 2, 1, 3)
        .reshape(map_rows, D)
    )
    full_order = part_orders(dp, fsdp)[0]
    all_heads = gather_doubling(own_heads, full_order)
    spot = inverse_place(full_order, dp, fsdp, dp_here, fsdp_here).reshape(-1)
    return block_grad, maps_grad, all_heads[spot].reshape(-1, BS), sums[-1], sums[:-1]


def norm_rows(inputs, gain_row, bias_row):
    center = inputs - jnp.mean(inputs, -1, keepdims=True)
    rstd = lax.rsqrt(jnp.mean(center * center, -1, keepdims=True) + norm_eps)
    scaled = center * rstd
    return scaled * gain_row + bias_row, scaled, rstd


def norm_rows_back(grad_out, scaled, rstd, gain_row):
    grad_scaled = grad_out * gain_row
    return rstd * (
        grad_scaled
        - jnp.mean(grad_scaled, -1, keepdims=True)
        - scaled * jnp.mean(grad_scaled * scaled, -1, keepdims=True)
    )


def dot32(left, right, ca, cb):
    return lax.dot_general(
        left, right, (((ca,), (cb,)), ((), ())), preferred_element_type=jnp.float32
    )


def model_kernel(fast, rows_of, *refs):
    refs = list(refs)
    take = lambda count: [refs.pop(0) for _ in range(count)]
    (owner, units, block_place, unit_place) = take(4)
    sources = take(12 if fast else 2)
    (hot, target, later_row, base, facts, legal, next_hot, act_hot, gains, head_w, head_b) = take(11)
    outs = take(6 if fast else 3)
    (sums_out,) = take(1)
    (wall, maps) = take(2)
    (normed1, qkv, probs, mixed, normed2, slope, act, final, grad_dyn, grad_head) = take(10)
    (grad_low, grad_pre, grad_mid, grad_qkv, grad_hid, small, bias_sum) = take(7)
    if fast:
        keep, send = take(2)
    wall_sem, maps_sem, out_sem = take(3)
    tokens = base.shape[0]
    tile = D // BS
    wide = FF // BS
    out_at = 3 * tile * tile
    expand_at = out_at + tile * tile
    contract_at = expand_at + tile * wide

    if fast:
        for part in range(3):
            for piece in range(4):
                source = sources[part * 4 + piece]

                def fetch(j, carry, part=part, piece=piece, source=source):
                    unit = units[part * 32 + piece * 8 + j]
                    for k in range(2):
                        block = owner[unit * 6 + part * 2 + k]
                        pltpu.make_async_copy(
                            source.at[j, k * BS : (k + 1) * BS, :], wall.at[block], wall_sem
                        ).start()
                    for i, chunk in enumerate(MAP_CHUNKS[part]):
                        pltpu.make_async_copy(
                            source.at[j, 2 * BS + i * 64 : 2 * BS + (i + 1) * 64, :],
                            maps.at[
                                pl.ds(pl.multiple_of(unit * 64, 64), 64),
                                chunk * BS : (chunk + 1) * BS,
                            ],
                            maps_sem,
                        ).start()
                    return carry

                lax.fori_loop(0, 8, fetch, 0)
    else:

        def fetch(j, carry):
            pltpu.make_async_copy(sources[0].at[j], wall.at[owner[j]], wall_sem).start()
            return carry

        lax.fori_loop(0, wall.shape[0], fetch, 0)
        pltpu.make_async_copy(sources[1], maps, maps_sem).start()
    small[...] = jnp.zeros_like(small)
    bias_sum[...] = jnp.zeros_like(bias_sum)
    sums_out[...] = jnp.zeros_like(sums_out)
    pltpu.make_async_copy(wall, wall, wall_sem).wait()
    pltpu.make_async_copy(maps, maps, maps_sem).wait()

    def grid_of(start, stride, row_count, col_count):
        return jnp.concatenate(
            [
                jnp.concatenate([wall[start + r * stride + c] for c in range(col_count)], 1)
                for r in range(row_count)
            ],
            0,
        )

    def chunk(step, carry):
        rows = pl.ds(pl.multiple_of(step * TM, TM), TM)
        hidden = dot32(hot[:, rows], maps[:LAT, :], 0, 0) + base[rows, :]
        normed, scaled1, rstd1 = norm_rows(hidden, gains[0:1], gains[1:2])
        normed1[rows, :] = normed.astype(jnp.bfloat16)

        def joint_strip(s, c):
            cols = pl.ds(pl.multiple_of(s * 256, 256), 256)
            weight = grid_of(2 * s, 3 * tile, tile, 2)
            qkv[rows, cols] = dot32(normed1[rows, :], weight, 1, 0).astype(jnp.bfloat16)
            return c

        lax.fori_loop(0, 6, joint_strip, 0)
        lane = lax.broadcasted_iota(jnp.int32, (BS, BS), 1)
        line = lax.broadcasted_iota(jnp.int32, (BS, BS), 0)
        allowed = (line >= lane) & (line // F == lane // F)
        low_half = lane < DH
        halves_of = [mask.astype(jnp.float32).astype(jnp.bfloat16) for mask in (low_half, ~low_half)]

        def attend(s, c):
            sub = pl.ds(pl.multiple_of(step * TM + s * BS, BS), BS)
            for pair in range(NH // 2):
                spans = [slice(part * D + pair * BS, part * D + (pair + 1) * BS) for part in range(3)]
                query, key, value = [qkv[sub, span] for span in spans]
                mixes = []
                for side in range(2):
                    half = halves_of[side]
                    scores = dot32(query * half, key, 1, 1) * DH ** (-0.5)
                    scores = jnp.where(allowed, scores, -1e30)
                    shifted = scores - jnp.max(scores, -1, keepdims=True)
                    power = jnp.exp(shifted)
                    prob = power / jnp.sum(power, -1, keepdims=True)
                    probs[2 * pair + side, sub, :] = prob
                    mixes.append(dot32(prob.astype(jnp.bfloat16), value, 1, 0))
                mixed[sub, pair * BS : (pair + 1) * BS] = jnp.where(low_half, *mixes).astype(
                    jnp.bfloat16
                )
            return c

        lax.fori_loop(0, TM // BS, attend, 0)
        out_map = grid_of(out_at, tile, tile, tile)
        middle = hidden + dot32(mixed[rows, :], out_map, 1, 0)
        normed, scaled2, rstd2 = norm_rows(middle, gains[2:3], gains[3:4])
        normed2[rows, :] = normed.astype(jnp.bfloat16)

        def expand_strip(s, c):
            cols = pl.ds(pl.multiple_of(s * 256, 256), 256)
            weight = grid_of(expand_at + 2 * s, wide, tile, 2)
            pre = dot32(normed2[rows, :], weight, 1, 0)
            square = pre * pre
            curve = jnp.tanh(GELU_A * (pre + GELU_B * (square * pre)))
            act[rows, cols] = (0.5 * pre * (1.0 + curve)).astype(jnp.bfloat16)
            slope[:, cols] = 0.5 * (1.0 + curve) + 0.5 * pre * (1.0 - curve * curve) * (
                GELU_A * (1.0 + 3.0 * GELU_B * square)
            )
            return c

        lax.fori_loop(0, FF // 256, expand_strip, 0)

        def contract_strip(s, total):
            cols = pl.ds(pl.multiple_of(s * 512, 512), 512)
            weight = grid_of(contract_at + s * 4 * tile, tile, 4, tile)
            return total + dot32(act[rows, cols], weight, 1, 0)

        top = lax.fori_loop(0, FF // 512, contract_strip, middle)
        normed, scaled3, rstd3 = norm_rows(top, gains[4:5], gains[5:6])
        final[rows, :] = normed.astype(jnp.bfloat16)
        late = later_row[0:1, rows]

        def dyn_strip(s, total):
            span = pl.ds(pl.multiple_of(s * 256, 256), 256)
            below = pl.ds(pl.multiple_of(LAT + s * 256, 256), 256)
            logits = dot32(maps[below, :], final[rows, :], 1, 1)
            logits = logits.reshape(256 // CLASSES, CLASSES, TM)
            shifted = logits - jnp.max(logits, 1, keepdims=True)
            power = jnp.exp(shifted)
            norm = jnp.sum(power, 1, keepdims=True)
            wanted = target[span, rows].astype(jnp.float32).reshape(256 // CLASSES, CLASSES, TM)
            spent = jnp.sum(wanted * (jnp.log(norm) - shifted), 0)
            grad = (power / norm - wanted) * late[None]
            grad_dyn[span, rows] = grad.reshape(256, TM).astype(jnp.bfloat16)
            return total + jnp.sum(spent, 0, keepdims=True) * late

        dyn_loss = lax.fori_loop(0, LAT // 256, dyn_strip, jnp.zeros((1, TM), jnp.float32))
        heads = dot32(final[rows, :], head_w[...], 1, 0) + head_b[0:1]
        now = facts[rows, 0:1]
        late_col = facts[rows, 1:2]
        spot = lax.broadcasted_iota(jnp.int32, (TM, 256), 1).astype(jnp.float32)
        frame_loss = jnp.zeros((TM, 1), jnp.float32)
        for which in range(2):
            logits = heads[:, which * 256 : (which + 1) * 256]
            bin_low = facts[rows, 2 + which : 3 + which]
            upper = facts[rows, 4 + which : 5 + which]
            weights = jnp.where(spot == bin_low, 1.0 - upper, 0.0)
            weights = weights + jnp.where(spot == bin_low + 1.0, upper, 0.0)
            shifted = logits - jnp.max(logits, -1, keepdims=True)
            power = jnp.exp(shifted)
            norm = jnp.sum(power, -1, keepdims=True)
            frame_loss = frame_loss + jnp.sum(
                weights * jnp.where(weights > 0.0, jnp.log(norm) - shifted, 0.0), -1, keepdims=True
            )
            grad = (power / norm - weights) * now
            grad_head[rows, which * 256 : (which + 1) * 256] = grad.astype(jnp.bfloat16)
            bias_sum[0:1, which * 256 : (which + 1) * 256] += jnp.sum(
                grad.astype(jnp.bfloat16).astype(jnp.float32), 0, keepdims=True
            )
        tail = heads[:, 512:640]
        logit = tail[:, 0:1]
        goal = facts[rows, 6:7]
        soft = jnp.maximum(logit, 0.0) + jnp.log1p(jnp.exp(-jnp.abs(logit)))
        frame_loss = (frame_loss + soft - goal * logit) * now
        may = legal[rows, :]
        chosen = next_hot[rows, :]
        masked = jnp.where(may > 0.5, tail, -1e30)
        shifted = masked - jnp.max(masked, -1, keepdims=True)
        power = jnp.exp(shifted)
        norm = jnp.sum(power, -1, keepdims=True)
        actor = jnp.sum(
            jnp.where(chosen > 0.5, jnp.log(norm) - shifted, 0.0), -1, keepdims=True
        )
        frame_loss = frame_loss + actor * late_col
        grad = (power / norm - chosen) * late_col
        column = lax.broadcasted_iota(jnp.int32, (TM, BS), 1)
        grad = jnp.where(column == 0, (jax.nn.sigmoid(logit) - goal) * now, grad)
        grad_head[rows, 512:640] = grad.astype(jnp.bfloat16)
        bias_sum[0:1, 512:640] += jnp.sum(
            grad.astype(jnp.bfloat16).astype(jnp.float32), 0, keepdims=True
        )
        sums_out[0:1, :] += jnp.broadcast_to(
            jnp.sum(dyn_loss, -1, keepdims=True) + jnp.sum(frame_loss, 0, keepdims=True), (1, BS)
        )
        sums_out[1:2, :] += jnp.broadcast_to(jnp.sum(now, 0, keepdims=True), (1, BS))

        grad_final = dot32(grad_dyn[:, rows], maps[LAT:, :], 0, 0) + dot32(
            grad_head[rows, :], head_w[...], 1, 1
        )
        small[4:5, :] += jnp.sum(grad_final * scaled3, 0, keepdims=True)
        small[5:6, :] += jnp.sum(grad_final, 0, keepdims=True)
        grad_top = norm_rows_back(grad_final, scaled3, rstd3, gains[4:5])
        grad_low[rows, :] = grad_top.astype(jnp.bfloat16)

        def act_strip(s, total):
            cols = pl.ds(pl.multiple_of(s * 256, 256), 256)
            weight = grid_of(contract_at + s * 2 * tile, tile, 2, tile)
            grad = dot32(grad_low[rows, :], weight, 1, 1) * slope[:, cols]
            grad = grad.astype(jnp.bfloat16)
            grad_pre[rows, cols] = grad
            weight = grid_of(expand_at + 2 * s, wide, tile, 2)
            return total + dot32(grad, weight, 1, 1)

        grad_normed = lax.fori_loop(
            0, FF // 256, act_strip, jnp.zeros((TM, D), jnp.float32)
        )
        small[2:3, :] += jnp.sum(grad_normed * scaled2, 0, keepdims=True)
        small[3:4, :] += jnp.sum(grad_normed, 0, keepdims=True)
        grad_middle = grad_top + norm_rows_back(grad_normed, scaled2, rstd2, gains[2:3])
        grad_mid[rows, :] = grad_middle.astype(jnp.bfloat16)
        out_map = grid_of(out_at, tile, tile, tile)
        mixed_grad = dot32(grad_mid[rows, :], out_map, 1, 1).astype(jnp.bfloat16)
        grad_hid[rows, :] = mixed_grad

        def attend_back(s, c):
            sub = pl.ds(pl.multiple_of(step * TM + s * BS, BS), BS)
            for pair in range(NH // 2):
                spans = [slice(part * D + pair * BS, part * D + (pair + 1) * BS) for part in range(3)]
                query, key, value = [qkv[sub, span] for span in spans]
                grad_out = grad_hid[sub, pair * BS : (pair + 1) * BS]
                totals = [jnp.zeros((BS, BS), jnp.float32) for _ in range(3)]
                for side in range(2):
                    half = halves_of[side]
                    prob = probs[2 * pair + side, sub, :]
                    out_half = grad_out * half
                    grad_prob = dot32(out_half, value, 1, 1)
                    dots = jnp.sum(grad_prob * prob, -1, keepdims=True)
                    grad_score = (prob * (grad_prob - dots)).astype(jnp.bfloat16)
                    totals[0] += dot32(grad_score, key * half, 1, 0)
                    totals[1] += dot32(grad_score, query * half, 0, 0)
                    totals[2] += dot32(prob.astype(jnp.bfloat16), out_half, 0, 0)
                for part, (span, total) in enumerate(zip(spans, totals)):
                    scale = DH ** (-0.5) if part < 2 else 1.0
                    grad_qkv[sub, span] = (total * scale).astype(jnp.bfloat16)
            return c

        lax.fori_loop(0, TM // BS, attend_back, 0)

        def joint_back(s, total):
            cols = pl.ds(pl.multiple_of(s * 512, 512), 512)
            weight = grid_of(4 * s, 3 * tile, tile, 4)
            return total + dot32(grad_qkv[rows, cols], weight, 1, 1)

        grad_normed = lax.fori_loop(0, 3, joint_back, jnp.zeros((TM, D), jnp.float32))
        small[0:1, :] += jnp.sum(grad_normed * scaled1, 0, keepdims=True)
        small[1:2, :] += jnp.sum(grad_normed, 0, keepdims=True)
        grad_in = grad_middle + norm_rows_back(grad_normed, scaled1, rstd1, gains[0:1])
        grad_hid[rows, :] = grad_in.astype(jnp.bfloat16)
        pieces = thirds(grad_in)
        small[...] += sum(dot32(act_hot[:, rows], piece, 1, 0) for piece in pieces)
        return carry

    lax.fori_loop(0, tokens // TM, chunk, 0)

    def put(place, rows, first, value):
        part = (place >> 8) & 3
        spot = place & 15
        dest = pl.ds(first, rows)

        @pl.when(((place >> 4) & 1) == 0)
        def _():
            keep[part, spot, dest, :] = value

        @pl.when(((place >> 4) & 1) == 1)
        def _():
            send[part, spot, dest, :] = value.astype(jnp.bfloat16)

    def put_block(block, value):
        place = block_place[block]
        if fast:
            put(place, BS, pl.multiple_of(((place >> 10) & 1) * BS, BS), value)
        else:
            outs[0][place] = value

    def block_grads(start, stride, left, right, row_count, col_steps):
        def strip(s, c):
            cols = pl.ds(pl.multiple_of(s * 256, 256), 256)
            grads = dot32(left, right[:, cols], 0, 0)
            for r in range(row_count):
                for k in range(2):
                    put_block(
                        start + r * stride + 2 * s + k,
                        grads[r * BS : (r + 1) * BS, k * BS : (k + 1) * BS],
                    )
            return c

        lax.fori_loop(0, col_steps, strip, 0)

    block_grads(0, 3 * tile, normed1[...], grad_qkv, tile, 6)
    block_grads(out_at, tile, mixed[...], grad_mid, tile, 2)
    block_grads(expand_at, wide, normed2[...], grad_pre, tile, FF // 256)

    def contract_rows(m, c):
        cols = pl.ds(pl.multiple_of(m * D, D), D)
        for s in range(2):
            grads = dot32(act[:, cols], grad_low[:, s * 256 : (s + 1) * 256], 0, 0)
            for r in range(tile):
                for k in range(2):
                    put_block(
                        contract_at + (m * tile + r) * tile + 2 * s + k,
                        grads[r * BS : (r + 1) * BS, k * BS : (k + 1) * BS],
                    )
        return c

    lax.fori_loop(0, FF // D, contract_rows, 0)

    def map_rows(m, c):
        span = pl.ds(pl.multiple_of(m * 256, 256), 256)
        for table in range(2):
            source, other = ((hot, grad_hid), (grad_dyn, final))[table]
            grads = dot32(source[span, :], other[...], 1, 0)
            if not fast:
                outs[1][pl.ds(pl.multiple_of(table * LAT + m * 256, 256), 256), :] = grads
                continue
            for u in range(4):
                unit = table * (LAT // 64) + m * 4 + u
                for part in range(3):
                    place = unit_place[part * 32 + unit]
                    for i, piece in enumerate(MAP_CHUNKS[part]):
                        put(
                            place,
                            64,
                            2 * BS + i * 64,
                            grads[u * 64 : (u + 1) * 64, piece * BS : (piece + 1) * BS],
                        )
        return c

    lax.fori_loop(0, LAT // 256, map_rows, 0)
    pieces = []
    for c in range(5):
        pieces.append(dot32(final[...], grad_head[:, c * BS : (c + 1) * BS], 0, 0))
    packed = jnp.concatenate(
        pieces
        + [
            bias_sum[0:1, c * BS : (c + 1) * BS] if c < 5 else jnp.zeros((3, BS), jnp.float32)
            for c in range(6)
        ]
        + [small[:, c * BS : (c + 1) * BS] for c in range(tile)]
        + [jnp.zeros((PACK_ROWS - 5 * D - 8 - tile * small.shape[0], BS), jnp.float32)],
        0,
    )
    if not fast:
        outs[2][...] = packed
        return
    for unit in range(32):
        for half in range(2):
            part = 1 + half
            place = unit_place[part * 32 + unit]
            first = unit * 96 + half * 48
            put(place, 48, 2 * BS + 64, packed[first : first + 48])
    copies = []
    for part in range(3):
        for which, scratch in enumerate((keep, send)):
            copies.append(
                pltpu.make_async_copy(
                    scratch.at[part, :, 0 : rows_of[part], :],
                    outs[part * 2 + which],
                    out_sem.at[part * 2 + which],
                )
            )
    for copy in copies:
        copy.start()
    for copy in copies:
        copy.wait()


def spread_cols(head):
    gap = jnp.zeros((head.shape[0], 1), head.dtype)
    rest = jnp.zeros((head.shape[0], BS - 1 - NA), head.dtype)
    return jnp.concatenate(
        [head[:, :BINS], gap, head[:, BINS : 2 * BINS], gap, head[:, 2 * BINS :], rest], 1
    )


def unpack_heads(packed, small_rows):
    chunks = [packed[c * D : (c + 1) * D] for c in range(5)]
    bias = jnp.concatenate([packed[5 * D + c : 5 * D + c + 1] for c in range(5)], 1)
    head = jnp.concatenate([jnp.concatenate(chunks, 1), bias], 0)
    head = jnp.concatenate(
        [head[:, :BINS], head[:, 256 : 256 + BINS], head[:, 512 : 513 + NA]], 1
    )
    start = 5 * D + 8
    small = jnp.concatenate(
        [packed[start + c * small_rows : start + (c + 1) * small_rows] for c in range(D // BS)], 1
    )
    return head, small


def model_grads(
    latents, actions, game_ids, action_masks, valid_steps, target_bins, target_fracs, continues,
    owner_order, blocks, latent_maps, head_weights, small_params, dp, fsdp,
):
    fast = (dp, fsdp) == (4, 8)
    seqs_here = latents.shape[0]
    tokens = seqs_here * F
    blocks_low = blocks.astype(jnp.bfloat16)
    maps_low = latent_maps.astype(jnp.bfloat16)
    inverse = jnp.argsort(owner_order).astype(jnp.int32)
    if fast:
        sources = gathered_pieces(blocks_low, maps_low, dp, fsdp)
        units, spots = placed_units(dp, fsdp)
        part_ids = jnp.arange(3)[:, None]
        unit_place = (part_ids << 8) + spots
        slot_unit = inverse // 6
        slot_part = inverse % 6 // 2
        block_place = ((inverse % 2) << 10) + unit_place.reshape(-1)[slot_part * (dp * fsdp) + slot_unit]
        units = units.reshape(-1).astype(jnp.int32)
        unit_place = unit_place.reshape(-1).astype(jnp.int32)
        block_place = block_place.astype(jnp.int32)
    else:
        sources = [
            lax.all_gather(blocks_low, "fsdp", axis=0, tiled=True),
            lax.all_gather(maps_low, "fsdp", axis=0, tiled=True),
        ]
        units = unit_place = jnp.zeros((96,), jnp.int32)
        block_place = inverse
    class_ids = jnp.arange(CLASSES)[None, :, None]

    def one_hot_rows(values):
        rows = values.reshape(tokens, GROUPS).T
        return (rows[:, None, :] == class_ids).astype(jnp.bfloat16).reshape(LAT, tokens)

    frame_last = (jnp.arange(F) < F - 1).astype(jnp.float32)[None, :]
    later = (jnp.roll(valid_steps, -1, axis=1).astype(jnp.float32) * frame_last).reshape(tokens)
    now = valid_steps.astype(jnp.float32).reshape(tokens)
    action_hot = (actions.reshape(tokens, 1) == jnp.arange(NA)[None, :]).astype(jnp.float32)
    base = jnp.dot(action_hot, small_params[4 * LAYERS + 2 :], precision=HIGHEST)
    base = (base.reshape(seqs_here, F, D) + positions(F, D)[None]).reshape(tokens, D)
    facts = jnp.concatenate(
        [
            now[:, None],
            later[:, None],
            target_bins.reshape(tokens, 2).astype(jnp.float32),
            target_fracs.reshape(tokens, 2),
            continues.reshape(tokens, 1).astype(jnp.float32),
            jnp.zeros((tokens, BS - 7), jnp.float32),
        ],
        1,
    )
    game_hot = (game_ids[:, None] == jnp.arange(NGAME)[None, :]).astype(jnp.float32)
    legal_rows = jnp.dot(game_hot, action_masks.astype(jnp.float32), precision=HIGHEST)
    legal = jnp.broadcast_to(legal_rows[:, None, :], (seqs_here, F, NA)).reshape(tokens, NA)
    legal = jnp.pad(legal, ((0, 0), (1, BS - 1 - NA)))
    next_hot = (
        jnp.roll(actions, -1, axis=1).reshape(tokens, 1) == jnp.arange(BS)[None, :] - 1
    ).astype(jnp.float32)
    small_rows = small_params.shape[0]
    act_hot = (
        jnp.arange(small_rows)[:, None] - (4 * LAYERS + 2) == actions.reshape(1, tokens)
    ).astype(jnp.bfloat16)
    gains = jnp.pad(small_params[: 4 * LAYERS + 2], ((0, 2), (0, 0)))
    head_wide = spread_cols(head_weights[:D].astype(jnp.bfloat16))
    column = jnp.arange(HEAD_COLS)[None, :]
    head_bias = jnp.where(
        (column == BINS) | (column == 256 + BINS), -1e30, spread_cols(head_weights[D:])
    )
    vmem = pl.BlockSpec(memory_space=pltpu.VMEM)
    smem = pl.BlockSpec(memory_space=pltpu.SMEM)
    away = pl.BlockSpec(memory_space=pl.ANY)
    low = jnp.bfloat16
    wide_type = jnp.float32
    if fast:
        shapes = []
        for rows in PART_ROWS:
            shapes += [((16, rows, BS), wide_type), ((16, rows, BS), low)]
        out_specs = [away] * 6 + [vmem]
    else:
        shapes = [
            (( 192, BS, BS), wide_type), ((2 * LAT, D), wide_type), ((PACK_ROWS, BS), wide_type)
        ]
        out_specs = [vmem] * 4
    shapes.append(((8, BS), wide_type))
    scratch = [
        pltpu.VMEM((owner_order.shape[0], BS, BS), low),
        pltpu.VMEM((2 * LAT, D), low),
        pltpu.VMEM((tokens, D), low),
        pltpu.VMEM((tokens, 3 * D), low),
        pltpu.VMEM((NH, tokens, BS), wide_type),
        pltpu.VMEM((tokens, D), low),
        pltpu.VMEM((tokens, D), low),
        pltpu.VMEM((TM, FF), wide_type),
        pltpu.VMEM((tokens, FF), low),
        pltpu.VMEM((tokens, D), low),
        pltpu.VMEM((LAT, tokens), low),
        pltpu.VMEM((tokens, HEAD_COLS), low),
        pltpu.VMEM((tokens, D), low),
        pltpu.VMEM((tokens, FF), low),
        pltpu.VMEM((tokens, D), low),
        pltpu.VMEM((tokens, 3 * D), low),
        pltpu.VMEM((tokens, D), low),
        pltpu.VMEM((small_rows, D), wide_type),
        pltpu.VMEM((8, HEAD_COLS), wide_type),
    ]
    if fast:
        scratch += [
            pltpu.VMEM((3, 16, PART_ROWS[0], BS), wide_type),
            pltpu.VMEM((3, 16, PART_ROWS[0], BS), low),
        ]
    scratch += [
        pltpu.SemaphoreType.DMA,
        pltpu.SemaphoreType.DMA,
        pltpu.SemaphoreType.DMA((6,)),
    ]
    *outs, sums = pl.pallas_call(
        functools.partial(model_kernel, fast, PART_ROWS),
        out_shape=[jax.ShapeDtypeStruct(shape, kind) for shape, kind in shapes],
        in_specs=[smem] * 4 + [away] * len(sources) + [vmem] * 11,
        out_specs=out_specs,
        scratch_shapes=scratch,
        compiler_params=pltpu.CompilerParams(vmem_limit_bytes=66 * 1000 * 1000),
        name="model",
    )(
        owner_order, units, block_place, unit_place, *sources,
        one_hot_rows(latents), one_hot_rows(jnp.roll(latents, -1, axis=1)),
        jnp.broadcast_to(later[None], (8, tokens)), base, facts, legal, next_hot, act_hot, gains,
        head_wide, jnp.broadcast_to(head_bias, (8, HEAD_COLS)),
    )
    return reduced_grads(outs, sums[:2, 0], blocks.shape[0], latent_maps.shape[0], dp, fsdp)


def thirds(value):
    first = value.astype(jnp.bfloat16)
    rest = value - first.astype(jnp.float32)
    second = rest.astype(jnp.bfloat16)
    third = (rest - second.astype(jnp.float32)).astype(jnp.bfloat16)
    return first, second, third


def stack_left(value, axis):
    a, b, c = thirds(value)
    return jnp.concatenate([a, a, b, a, b, c], axis)


def stack_right(value, axis):
    a, b, c = thirds(value)
    return jnp.concatenate([a, b, a, c, b, a], axis)


def fdot(left, right, ca, cb):
    return lax.dot_general(
        stack_left(left, ca),
        stack_right(right, cb),
        (((ca,), (cb,)), ((), ())),
        preferred_element_type=jnp.float32,
    )


def qr_kernel(count, stat_ref, basis_ref, out_ref, work):
    tiles = -(-count // PACK)
    rows = PACK * PAN
    panels = BS // PAN

    batch = next(size for size in (8, 6, 4, 3, 2, 1) if count % size == 0)

    def start(step, _):
        ids = [step * batch + c for c in range(batch)]
        stats = [stat_ref[b] for b in ids]
        bases = [basis_ref[b] for b in ids]
        scales = [
            1.0 / jnp.max(jnp.sum(jnp.abs(stat), -1, keepdims=True), 0, keepdims=True)
            for stat in stats
        ]
        xts = [fdot(base, stat, 0, 0) * scale for base, stat, scale in zip(bases, stats, scales)]
        grams = [fdot(xt, xt, 1, 1) for xt in xts]
        for b, xt, gram in zip(ids, xts, grams):
            for p in range(panels):
                work[p, pl.ds(b * PAN, PAN), :BS] = gram[p * PAN : (p + 1) * PAN]
                work[p, pl.ds(b * PAN, PAN), BS:] = xt[p * PAN : (p + 1) * PAN]
        return _

    lax.fori_loop(0, count // batch, start, 0)
    row_id = lax.broadcasted_iota(jnp.int32, (PAN, BS), 0)
    lane_id = lax.broadcasted_iota(jnp.int32, (PAN, BS), 1)
    group = lane_id // PAN
    for p in range(panels):
        packed = []
        for t in range(tiles):
            tile = jnp.zeros((PAN, BS), jnp.float32)
            for c in range(PACK):
                b = t * PACK + c
                if b < count:
                    diag = work[p, b * PAN : (b + 1) * PAN, :BS]
                    shift = (c - p) * PAN % BS
                    if shift:
                        diag = pltpu.roll(diag, shift, 1)
                    tile = jnp.where(group == c, diag, tile)
                else:
                    tile = jnp.where((group == c) & (lane_id % PAN == row_id), 1.0, tile)
            packed.append(tile)
        inverse = [jnp.where(lane_id % PAN == row_id, 1.0, 0.0) for _ in range(tiles)]
        scales = [jnp.ones((PAN, BS), jnp.float32) for _ in range(tiles)]
        for k in range(PAN):
            index = group * PAN + k
            for t in range(tiles):
                tile = packed[t]
                column = jnp.take_along_axis(tile, index, axis=1, mode="promise_in_bounds")
                pivot = column[k : k + 1]
                scales[t] = jnp.where(row_id == k, lax.rsqrt(pivot), scales[t])
                if k < PAN - 1:
                    factor = jnp.where(row_id > k, column * (1.0 / pivot), 0.0)
                    packed[t] = tile - factor * tile[k : k + 1]
                    inverse[t] = inverse[t] - factor * inverse[t][k : k + 1]
        for t in range(tiles):
            low = inverse[t] * scales[t]
            spread = jnp.concatenate([jnp.where(group == c, low, 0.0) for c in range(PACK)], 0)
            here = min(rows, (count - t * PACK) * PAN)
            spread = spread[:here]
            if here < rows:
                spread = spread[:, :here]
            span = slice(t * rows, t * rows + here)
            work[p, span, :] = fdot(spread, work[p, span, :], 1, 0)
        if p < panels - 1:

            def trail(step, _, p=p):
                ids = [step * batch + c for c in range(batch)]
                uppers = [work[p, pl.ds(b * PAN, PAN), :] for b in ids]
                changes = [fdot(upper[:, :BS], upper, 0, 0) for upper in uppers]
                for b, change in zip(ids, changes):
                    for q in range(p + 1, panels):
                        work[q, pl.ds(b * PAN, PAN), :] -= change[q * PAN : (q + 1) * PAN]
                return _

            lax.fori_loop(0, count // batch, trail, 0)

    def finish(b, _):
        rows_q = jnp.concatenate([work[p, pl.ds(b * PAN, PAN), BS:] for p in range(panels)], 0)
        out_ref[b] = rows_q.T
        return _

    lax.fori_loop(0, count, finish, 0, unroll=2)


def renew_all(stats, bases):
    count = stats.shape[0]
    return pl.pallas_call(
        functools.partial(qr_kernel, count),
        out_shape=jax.ShapeDtypeStruct((count, BS, BS), jnp.float32),
        in_specs=[pl.BlockSpec(memory_space=pltpu.VMEM)] * 2,
        out_specs=pl.BlockSpec(memory_space=pltpu.VMEM),
        scratch_shapes=[pltpu.VMEM((BS // PAN, count * PAN, 2 * BS), jnp.float32)],
        name="renew",
    )(stats, bases)


def soap_update(weight, first_moment, second_moment, left, right, left_rot, right_rot, grad):
    left = beta_two * left + (1.0 - beta_two) * jnp.einsum(
        "bij,bkj->bik", grad, grad, precision=HIGHEST
    )
    right = beta_two * right + (1.0 - beta_two) * jnp.einsum(
        "bji,bjk->bik", grad, grad, precision=HIGHEST
    )
    rotated = jnp.einsum("bji,bjk->bik", left_rot, grad, precision=HIGHEST)
    rotated = jnp.einsum("bij,bjk->bik", rotated, right_rot, precision=HIGHEST)
    first_moment = beta_one * first_moment + (1.0 - beta_one) * rotated
    second_moment = beta_two * second_moment + (1.0 - beta_two) * rotated * rotated
    direction = (
        first_moment
        / (1.0 - beta_one**STEP)
        / (jnp.sqrt(second_moment / (1.0 - beta_two**STEP)) + epsilon)
    )
    direction = jnp.einsum("bij,bjk->bik", left_rot, direction, precision=HIGHEST)
    direction = jnp.einsum("bij,bkj->bik", direction, right_rot, precision=HIGHEST)
    weight = weight - learn_rate * (direction + weight_decay * weight)
    count = weight.shape[0]
    renewed = renew_all(
        jnp.concatenate([left, right], 0), jnp.concatenate([left_rot, right_rot], 0)
    )
    return (
        weight,
        first_moment,
        second_moment,
        left,
        right,
        renewed[:count],
        renewed[count:],
    )


def adam_update(weight, first_moment, second_moment, grad, decay_rate, rate):
    first_moment = beta_one * first_moment + (1.0 - beta_one) * grad
    second_moment = beta_two * second_moment + (1.0 - beta_two) * grad * grad
    direction = (
        first_moment
        / (1.0 - beta_one**STEP)
        / (jnp.sqrt(second_moment / (1.0 - beta_two**STEP)) + epsilon)
    )
    return (weight - rate * (direction + decay_rate * weight), first_moment, second_moment)


def shards(
    latents,
    actions,
    game_ids,
    action_masks,
    valid_steps,
    target_bins,
    target_fracs,
    continues,
    owner_order,
    blocks,
    block_first,
    block_second,
    left_stat,
    right_stat,
    left_basis,
    right_basis,
    latent_maps,
    latent_first,
    latent_second,
    head_weights,
    head_first,
    head_second,
    small_params,
    small_first,
    small_second,
    ema_critic,
    dp,
    fsdp,
):
    block_grad, maps_grad, packed_grad, square, sums = model_grads(
        latents, actions, game_ids, action_masks, valid_steps, target_bins, target_fracs, continues,
        owner_order, blocks, latent_maps, head_weights, small_params, dp, fsdp,
    )
    head_grad, small_grad = unpack_heads(packed_grad, small_params.shape[0])
    counted = sums[1]
    loss_value = sums[0] / counted
    grad_norm = jnp.sqrt(square) / counted
    factor = jnp.minimum(1.0, clip_norm / grad_norm) / counted
    soap_out = soap_update(
        blocks,
        block_first,
        block_second,
        left_stat,
        right_stat,
        left_basis,
        right_basis,
        block_grad * factor,
    )
    maps_out = adam_update(
        latent_maps, latent_first, latent_second, maps_grad * factor, weight_decay, learn_rate
    )
    heads_out = adam_update(
        head_weights, head_first, head_second, head_grad * factor, weight_decay, learn_rate
    )
    small_out = adam_update(
        small_params, small_first, small_second, small_grad * factor, 0.0, small_rate
    )
    ema_new = ema_rate * ema_critic + (1.0 - ema_rate) * heads_out[0][:, BINS : 2 * BINS]
    return (
        loss_value,
        grad_norm,
        soap_out[0],
        soap_out[1],
        soap_out[2],
        soap_out[3],
        soap_out[4],
        soap_out[5],
        soap_out[6],
        maps_out[0],
        maps_out[1],
        maps_out[2],
        heads_out[0],
        heads_out[1],
        heads_out[2],
        small_out[0],
        small_out[1],
        small_out[2],
        ema_new,
    )


def solution(mesh):
    placed = (
        P(("dp", "fsdp"), None, None),
        P(("dp", "fsdp"), None),
        P(("dp", "fsdp")),
        P(),
        P(("dp", "fsdp"), None),
        P(("dp", "fsdp"), None, None),
        P(("dp", "fsdp"), None, None),
        P(("dp", "fsdp"), None),
        P(),
        P("fsdp", None, None),
        P("fsdp", None, None),
        P("fsdp", None, None),
        P("fsdp", None, None),
        P("fsdp", None, None),
        P("fsdp", None, None),
        P("fsdp", None, None),
        P("fsdp", None),
        P("fsdp", None),
        P("fsdp", None),
        P(),
        P(),
        P(),
        P(),
        P(),
        P(),
        P(),
    )
    return jax.shard_map(
        functools.partial(shards, dp=mesh.shape["dp"], fsdp=mesh.shape["fsdp"]),
        mesh=mesh,
        in_specs=placed,
        out_specs=(
            P(),
            P(),
            P("fsdp", None, None),
            P("fsdp", None, None),
            P("fsdp", None, None),
            P("fsdp", None, None),
            P("fsdp", None, None),
            P("fsdp", None, None),
            P("fsdp", None, None),
            P("fsdp", None),
            P("fsdp", None),
            P("fsdp", None),
            P(),
            P(),
            P(),
            P(),
            P(),
            P(),
            P(),
        ),
        check_vma=False,
    )
```

profile of v0, /device:TPU:0, one launch (start us, length us, event | category | flops | bytes accessed | tf_op | source)
XLA Modules:
  0.0 370.9 jit_solution(12569286250642179275)
XLA Ops:
  0.7 1.1 dynamic-slice_convert_fusion
  2.9 4.1 %collective-permute-start.12 = (bf16[1,320,128]{2,1,0:T(8,128)(2,1)S(1)}, bf16[1,320,128]{2,1,0:T(8,128)(2,1)S(1)}, u32[]{:S(2)}, u32[]{:S(2)}) collective-permute-start(bf16[1,320,128]{2,1,0:T(8,128)(2,1)S(1)} %maximum_bitcast_fusion.2), channel_id=1, source_target_pairs={{0,4},{1,5},{2,6},{3,7},{4,0},{5,1},{6,2},{7,3},{8,12},{9,13},{10,... | collective-permute-start | bytes 245768 | tf_op jit(solution)/shard_map/ppermute | solution.py:61
  7.0 1.5 collective-permute-start.6
  9.8 3.2 sort.17
  13.1 1.6 gather_fusion
  17.2 1.4 slice_select_fusion.refs_24_
  18.7 1.6 collective-permute-start.1
  20.4 1.6 collective-permute-start.13
  21.9 2.7 collective-permute-start.7
  24.6 1.3 collective-permute-done.1
  25.9 2.9 collective-permute-start.2
  29.5 1.6 collective-permute-done.7
  31.2 3.3 collective-permute-done.2
  35.2 4.1 %collective-permute-done.14 = bf16[4,320,128]{2,1,0:T(8,128)(2,1)S(1)} collective-permute-done((bf16[4,320,128]{2,1,0:T(8,128)(2,1)S(1)}, bf16[4,320,128]{2,1,0:T(8,128)(2,1)S(1)}, u32[]{:S(2)}, u32[]{:S(2)}) %collective-permute-start.14) | collective-permute-done | bytes 327712 | tf_op jit(solution)/shard_map/ppermute | solution.py:61
  39.6 2.2 collective-permute-done.8
  42.8 1.2 fusion.20
  44.9 8.2 %collective-permute-done.3.refs_5_ = bf16[8,384,128]{2,1,0:T(8,128)(2,1)} collective-permute-done((bf16[8,384,128]{2,1,0:T(8,128)(2,1)S(1)}, bf16[8,384,128]{2,1,0:T(8,128)(2,1)}, u32[]{:S(2)}, u32[]{:S(2)}) %collective-permute-start.3) | collective-permute-done | bytes 786464 | tf_op jit(solution)/shard_map/ppermute | solution.py:61
  53.8 3.3 collective-permute-done.9.refs_9_
  60.9 1.7 fusion.1
  62.7 2.0 concatenate.145.refs_25_
  64.7 1.1 concatenate.143.refs_20_
  66.8 1.6 convolution_add_fusion.refs_19_
  69.7 82.8 %model.1 = (f32[16,384,128]{2,1,0:T(8,128)}, bf16[16,384,128]{2,1,0:T(8,128)(2,1)}, f32[16,368,128]{2,1,0:T(8,128)}, bf16[16,368,128]{2,1,0:T(8,128)(2,1)}, f32[...) custom-call(s32[192]{0:T(256)} %refs_0_.1, s32[96]{0:T(128)} %reshape.901.refs_1_, ...), custom_call_target="tpu_custom_call" | custom-call | tf_op jit(solution)/shard_map/model/pallas_call | solution.py:739
  153.8 4.2 %pad_maximum_fusion.1.basis_ref = f32[48,128,128]{2,1,0:T(8,128)} fusion(f32[24,128,128]{2,1,0:T(8,128)} %param.41, f32[24,128,128]{2,1,0:T(8,128)} %param.40), kind=kLoop, calls=%fused_computation.4 | loop fusion | flops 786432 | bytes 6291456 | tf_op jit(solution)/shard_map/concatenate | solution.py:901
  157.9 1.8 convert_add_fusion.1
  159.9 2.0 collective-permute-start.29
  164.9 14.1 %collective-permute-done.29 = bf16[8,368,128]{2,1,0:T(8,128)(2,1)S(1)} collective-permute-done((bf16[8,368,128]{2,1,0:T(8,128)(2,1)S(1)}, bf16[8,368,128]{2,1,0:T(8,128)(2,1)S(1)}, u32[]{:S(2)}, u32[]{:S(2)}) %collective-permute-start.29) | collective-permute-done | bytes 753696 | tf_op jit(solution)/shard_map/ppermute | solution.py:61
  179.7 1.2 collective-permute-done.24
  181.7 3.0 collective-permute-done.19
  185.7 6.0 %collective-permute-done.30 = bf16[4,368,128]{2,1,0:T(8,128)(2,1)S(1)} collective-permute-done((bf16[4,368,128]{2,1,0:T(8,128)(2,1)S(1)}, bf16[4,368,128]{2,1,0:T(8,128)(2,1)S(1)}, u32[]{:S(2)}, u32[]{:S(2)}) %collective-permute-start.30) | collective-permute-done | bytes 376864 | tf_op jit(solution)/shard_map/ppermute | solution.py:61
  192.3 1.4 collective-permute-start.26
  195.4 6.5 %collective-permute-done.31 = f32[2,368,128]{2,1,0:T(8,128)S(1)} collective-permute-done((f32[2,368,128]{2,1,0:T(8,128)S(1)}, f32[2,368,128]{2,1,0:T(8,128)S(1)}, u32[]{:S(2)}, u32[]{:S(2)}) %collective-permute-start.31) | collective-permute-done | bytes 376864 | tf_op jit(solution)/shard_map/ppermute | solution.py:61
  202.3 10.5 %collective-permute-done.26 = f32[2,368,128]{2,1,0:T(8,128)S(1)} collective-permute-done((f32[2,368,128]{2,1,0:T(8,128)S(1)}, f32[2,368,128]{2,1,0:T(8,128)S(1)}, u32[]{:S(2)}, u32[]{:S(2)}) %collective-permute-start.26) | collective-permute-done | bytes 376864 | tf_op jit(solution)/shard_map/ppermute | solution.py:61
  214.0 9.3 %collective-permute-done.32 = f32[1,368,128]{2,1,0:T(8,128)S(1)} collective-permute-done((f32[1,368,128]{2,1,0:T(8,128)S(1)}, f32[1,368,128]{2,1,0:T(8,128)S(1)}, u32[]{:S(2)}, u32[]{:S(2)}) %collective-permute-start.32) | collective-permute-done | bytes 188448 | tf_op jit(solution)/shard_map/ppermute | solution.py:61
  225.3 4.3 %collective-permute-done.40 = f32[1,96,128]{2,1,0:T(8,128)S(1)} collective-permute-done((f32[1,96,128]{2,1,0:T(8,128)S(1)}, f32[1,96,128]{2,1,0:T(8,128)S(1)}, u32[]{:S(2)}, u32[]{:S(2)}) %collective-permute-start.40) | collective-permute-done | bytes 49184 | tf_op jit(solution)/shard_map/ppermute | solution.py:61
  231.1 3.2 collective-permute-done.41
  234.4 1.7 collective-permute-start.42
  236.1 4.0 %collective-permute-done.42 = f32[4,96,128]{2,1,0:T(8,128)S(1)} collective-permute-done((f32[4,96,128]{2,1,0:T(8,128)S(1)}, f32[4,96,128]{2,1,0:T(8,128)S(1)}, u32[]{:S(2)}, u32[]{:S(2)}) %collective-permute-start.42) | collective-permute-done | bytes 196640 | tf_op jit(solution)/shard_map/ppermute | solution.py:61
  240.1 1.5 collective-permute-start.43
  243.1 4.9 %collective-permute-done.43 = f32[8,96,128]{2,1,0:T(8,128)S(1)} collective-permute-done((f32[8,96,128]{2,1,0:T(8,128)S(1)}, f32[8,96,128]{2,1,0:T(8,128)S(1)}, u32[]{:S(2)}, u32[]{:S(2)}) %collective-permute-start.43) | collective-permute-done | bytes 393248 | tf_op jit(solution)/shard_map/ppermute | solution.py:61
  248.9 1.5 collective-permute-start.38
  255.1 8.3 %collective-permute-done.34 = f32[3]{0:T(128)S(1)} collective-permute-done((f32[3]{0:T(128)S(1)}, f32[3]{0:T(128)S(1)}, u32[]{:S(2)}, u32[]{:S(2)}) %collective-permute-start.34) | collective-permute-done | bytes 44 | tf_op jit(solution)/shard_map/ppermute | solution.py:61
  263.4 1.7 collective-permute-start.35
  265.1 1.9 collective-permute-done.35
  267.2 3.3 collective-permute-done.36
  271.5 3.5 collective-permute-done.37
  281.7 2.1 gather_fusion.2
  286.0 2.8 multiply_subtract_fusion.1
  288.8 1.2 fusion.17
  290.1 1.4 pad_maximum_fusion.2
  291.4 2.0 gather_fusion.1
  294.5 1.6 slice_multiply_fusion
  296.2 1.1 copy.57
  297.3 2.7 fusion.72
  300.0 3.0 multiply_add_fusion
  303.0 3.4 multiply_add_fusion.1
  306.5 1.1 copy-done.4
  307.6 2.0 pad_maximum_fusion.stat_ref
  309.6 43.9 %renew.1 = f32[48,128,128]{2,1,0:T(8,128)} custom-call(f32[48,128,128]{2,1,0:T(8,128)} %pad_maximum_fusion.stat_ref, f32[48,128,128]{2,1,0:T(8,128)} %pad_maximum_fusion.1.basis_ref), custom_call_target="tpu_custom_call" | custom-call | tf_op jit(solution)/shard_map/renew/pallas_call | solution.py:870
  353.5 4.0 %fusion.66 = (f32[24,128,128]{2,1,0:T(8,128)}, f32[24,128,128]{2,1,0:T(8,128)}) fusion(f32[48,128,128]{2,1,0:T(8,128)} %renew.1), kind=kLoop, calls=%fused_computation.256 | loop fusion | bytes 6291456 | tf_op jit(solution)/shard_map/slice | solution.py:910
  357.6 2.2 multiply_add_fusion.2
  359.9 2.5 fusion.3
  362.4 4.6 %multiply_subtract_fusion = f32[24,128,128]{2,1,0:T(8,128)} fusion(f32[24,128,128]{2,1,0:T(8,128)S(1)} %copy-done.15, f32[24,128,128]{1,2,0:T(8,128)S(1)} %fusion.3, f32[24,128,128]{2,1,0:T(8,128)S(1)} %copy-done.1), kind=kOutput, calls=%fused_computation.23 | convolution fusion | flops 605552640 | bytes 6291456 | tf_op jit(solution)/shard_map/bij,bkj->bik/dot_general | solution.py:897
  367.0 1.4 multiply_subtract_fusion.2
  (301 shorter events, 41.7 us)
Async XLA Ops:
  0.7 8.4 %copy-start.5 = (f32[513,529]{1,0:T(8,128)S(1)}, f32[513,529]{1,0:T(8,128)}, u32[]{:S(2)}) copy-start(f32[513,529]{1,0:T(8,128)} %param.45) | copy-start | bytes 3256528
  0.7 8.5 %copy-start.36 = (s32[8,64]{1,0:T(8,128)S(1)}, s32[8,64]{1,0:T(8,128)}, u32[]{:S(2)}) copy-start(s32[8,64]{1,0:T(8,128)} %param.27) | copy-start | bytes 6148
  0.7 9.2 %copy-start.40 = (s32[192]{0:T(256)S(1)}, s32[192]{0:T(256)}, u32[]{:S(2)}) copy-start(s32[192]{0:T(256)} %refs_0_.1) | copy-start | bytes 2308
  0.7 14.6 %copy-start.24 = (s32[8,64,32]{1,2,0:T(8,128)S(1)}, s32[8,64,32]{1,2,0:T(8,128)}, u32[]{:S(2)}) copy-start(s32[8,64,32]{1,2,0:T(8,128)} %param.26) | copy-start | bytes 196612
  0.7 14.7 %copy-start.37 = (s32[8,64]{1,0:T(8,128)S(1)}, s32[8,64]{1,0:T(8,128)}, u32[]{:S(2)}) copy-start(s32[8,64]{1,0:T(8,128)} %param.30) | copy-start | bytes 6148
  1.8 15.1 %copy-start.43 = (s32[26,18]{0,1:T(8,128)S(1)}, s32[26,18]{0,1:T(8,128)}, u32[]{:S(2)}) copy-start(s32[26,18]{0,1:T(8,128)} %param.29) | copy-start | bytes 5620
  1.9 15.1 %copy-start.44 = (s32[8]{0:T(128)S(1)}, s32[8]{0:T(128)}, u32[]{:S(2)}) copy-start(s32[8]{0:T(128)} %param.28) | copy-start | bytes 100
  1.9 15.3 %copy-start.42 = (pred[8]{0:T(512)(128)(4,1)S(1)}, pred[8]{0:T(512)(128)(4,1)}, u32[]{:S(2)}) copy-start(pred[8]{0:T(512)(128)(4,1)} %constant.253.clone.1) | copy-start | bytes 28
  2.9 17.5 %collective-permute-start.12 = (bf16[1,320,128]{2,1,0:T(8,128)(2,1)S(1)}, bf16[1,320,128]{2,1,0:T(8,128)(2,1)S(1)}, u32[]{:S(2)}, u32[]{:S(2)}) collective-permute-start(bf16[1,320,128]{2,1,0:T(8,128)(2,1)S(1)} %maximum_bitcast_fusion.2), channel_id=1, source_target_pairs={{0,4},{1,5},{2,6},{3,7},{4,0},{5,1},{6,2},{7,3},{8,12},{9,13},{10,... | collective-permute-start | bytes 245768 | tf_op jit(solution)/shard_map/ppermute | solution.py:61
  7.0 14.9 %collective-permute-start.6 = (bf16[1,320,128]{2,1,0:T(8,128)(2,1)S(1)}, bf16[1,320,128]{2,1,0:T(8,128)(2,1)S(1)}, u32[]{:S(2)}, u32[]{:S(2)}) collective-permute-start(bf16[1,320,128]{2,1,0:T(8,128)(2,1)S(1)} %maximum_bitcast_fusion.1), channel_id=1, source_target_pairs={{0,16},{8,24},{16,0},{24,8},{1,17},{9,25},{17,1},{25,9},{2,18},{10... | collective-permute-start | bytes 245768 | tf_op jit(solution)/shard_map/ppermute | solution.py:61
  8.5 10.1 %collective-permute-start = (bf16[1,384,128]{2,1,0:T(8,128)(2,1)S(1)}, bf16[1,384,128]{2,1,0:T(8,128)(2,1)S(1)}, u32[]{:S(2)}, u32[]{:S(2)}) collective-permute-start(bf16[1,384,128]{2,1,0:T(8,128)(2,1)S(1)} %maximum_bitcast_fusion), channel_id=1, source_target_pairs={{0,4},{1,5},{2,6},{3,7},{4,0},{5,1},{6,2},{7,3},{8,12},{9,13},{10,... | collective-permute-start | bytes 294920 | tf_op jit(solution)/shard_map/ppermute | solution.py:61
  9.8 16.1 %copy-start = (s32[96]{0:T(128)}, s32[96]{0:T(128)S(1)}, u32[]{:S(2)}) copy-start(s32[96]{0:T(128)S(1)} %add.712.refs_3_) | copy-start | bytes 1156
  18.7 7.2 %collective-permute-start.1 = (bf16[2,384,128]{2,1,0:T(8,128)(2,1)S(1)}, bf16[2,384,128]{2,1,0:T(8,128)(2,1)S(1)}, u32[]{:S(2)}, u32[]{:S(2)}) collective-permute-start(bf16[2,384,128]{2,1,0:T(8,128)(2,1)S(1)} %pad_maximum_fusion.11), channel_id=1, source_target_pairs={{0,2},{1,3},{2,0},{3,1},{4,6},{5,7},{6,4},{7,5},{8,10},{9,11},{10,... | collective-permute-start | bytes 589832 | tf_op jit(solution)/shard_map/ppermute | solution.py:61
  20.4 8.5 %collective-permute-start.13 = (bf16[2,320,128]{2,1,0:T(8,128)(2,1)S(1)}, bf16[2,320,128]{2,1,0:T(8,128)(2,1)S(1)}, u32[]{:S(2)}, u32[]{:S(2)}) collective-permute-start(bf16[2,320,128]{2,1,0:T(8,128)(2,1)S(1)} %pad_maximum_fusion.14), channel_id=1, source_target_pairs={{0,1},{1,0},{2,3},{3,2},{4,5},{5,4},{6,7},{7,6},{8,9},{9,8},{10,11... | collective-permute-start | bytes 491528 | tf_op jit(solution)/shard_map/ppermute | solution.py:61
  21.9 9.2 %collective-permute-start.7 = (bf16[2,320,128]{2,1,0:T(8,128)(2,1)S(1)}, bf16[2,320,128]{2,1,0:T(8,128)(2,1)S(1)}, u32[]{:S(2)}, u32[]{:S(2)}) collective-permute-start(bf16[2,320,128]{2,1,0:T(8,128)(2,1)S(1)} %pad_maximum_fusion.13), channel_id=1, source_target_pairs={{0,4},{1,5},{2,6},{3,7},{4,0},{5,1},{6,2},{7,3},{8,12},{9,13},{10,... | collective-permute-start | bytes 491528 | tf_op jit(solution)/shard_map/ppermute | solution.py:61
  25.9 8.7 %collective-permute-start.2 = (bf16[4,384,128]{2,1,0:T(8,128)(2,1)S(1)}, bf16[4,384,128]{2,1,0:T(8,128)(2,1)S(1)}, u32[]{:S(2)}, u32[]{:S(2)}) collective-permute-start(bf16[4,384,128]{2,1,0:T(8,128)(2,1)S(1)} %pad_maximum_fusion.7), channel_id=1, source_target_pairs={{0,1},{1,0},{2,3},{3,2},{4,5},{5,4},{6,7},{7,6},{8,9},{9,8},{10,11... | collective-permute-start | bytes 1179656 | tf_op jit(solution)/shard_map/ppermute | solution.py:61
  29.0 10.4 %collective-permute-start.14 = (bf16[4,320,128]{2,1,0:T(8,128)(2,1)S(1)}, bf16[4,320,128]{2,1,0:T(8,128)(2,1)S(1)}, u32[]{:S(2)}, u32[]{:S(2)}) collective-permute-start(bf16[4,320,128]{2,1,0:T(8,128)(2,1)S(1)} %pad_maximum_fusion.10), channel_id=1, source_target_pairs={{0,16},{8,24},{16,0},{24,8},{1,17},{9,25},{17,1},{25,9},{2,18},{10... | collective-permute-start | bytes 983048 | tf_op jit(solution)/shard_map/ppermute | solution.py:61
  31.1 10.6 %collective-permute-start.8 = (bf16[4,320,128]{2,1,0:T(8,128)(2,1)S(1)}, bf16[4,320,128]{2,1,0:T(8,128)(2,1)S(1)}, u32[]{:S(2)}, u32[]{:S(2)}) collective-permute-start(bf16[4,320,128]{2,1,0:T(8,128)(2,1)S(1)} %pad_maximum_fusion.9), channel_id=1, source_target_pairs={{0,2},{1,3},{2,0},{3,1},{4,6},{5,7},{6,4},{7,5},{8,10},{9,11},{10,... | collective-permute-start | bytes 983048 | tf_op jit(solution)/shard_map/ppermute | solution.py:61
  34.7 10.2 %copy-start.7 = (bf16[8,384,128]{2,1,0:T(8,128)(2,1)}, bf16[8,384,128]{2,1,0:T(8,128)(2,1)S(1)}, u32[]{:S(2)}) copy-start(bf16[8,384,128]{2,1,0:T(8,128)(2,1)S(1)} %pad_maximum_fusion.4.refs_4_) | copy-start | bytes 2359300
  34.7 18.4 %collective-permute-start.3 = (bf16[8,384,128]{2,1,0:T(8,128)(2,1)S(1)}, bf16[8,384,128]{2,1,0:T(8,128)(2,1)}, u32[]{:S(2)}, u32[]{:S(2)}) collective-permute-start(bf16[8,384,128]{2,1,0:T(8,128)(2,1)S(1)} %pad_maximum_fusion.4.refs_4_), channel_id=1, source_target_pairs={{0,16},{8,24},{16,0},{24,8},{1,17},{9,25},{17,1},{25,9},{2,18},{10... | collective-permute-start | bytes 2359304 | tf_op jit(solution)/shard_map/ppermute | solution.py:61
  39.4 18.4 %copy-start.11 = (bf16[8,320,128]{2,1,0:T(8,128)(2,1)}, bf16[8,320,128]{2,1,0:T(8,128)(2,1)S(1)}, u32[]{:S(2)}) copy-start(bf16[8,320,128]{2,1,0:T(8,128)(2,1)S(1)} %pad_maximum_fusion.6.refs_12_) | copy-start | bytes 1966084
  39.5 19.3 %copy-start.30 = (s32[8,64,32]{1,2,0:T(8,128)S(1)}, s32[8,64,32]{1,2,0:T(8,128)}, u32[]{:S(2)}) copy-start(s32[8,64,32]{1,2,0:T(8,128)} %pad_add_fusion) | copy-start | bytes 196612
  39.5 13.6 %collective-permute-start.15 = (bf16[8,320,128]{2,1,0:T(8,128)(2,1)S(1)}, bf16[8,320,128]{2,1,0:T(8,128)(2,1)}, u32[]{:S(2)}, u32[]{:S(2)}) collective-permute-start(bf16[8,320,128]{2,1,0:T(8,128)(2,1)S(1)} %pad_maximum_fusion.6.refs_12_), channel_id=1, source_target_pairs={{0,2},{1,3},{2,0},{3,1},{4,6},{5,7},{6,4},{7,5},{8,10},{9,11},{10,... | collective-permute-start | bytes 1966088 | tf_op jit(solution)/shard_map/ppermute | solution.py:61
  39.5 14.1 %collective-permute-start.16 = (bf16[8,320,128]{2,1,0:T(8,128)(2,1)S(1)}, bf16[8,320,128]{2,1,0:T(8,128)(2,1)S(1)}, u32[]{:S(2)}, u32[]{:S(2)}) collective-permute-start(bf16[8,320,128]{2,1,0:T(8,128)(2,1)S(1)} %pad_maximum_fusion.6.refs_12_), channel_id=1, source_target_pairs={{0,8},{8,0},{16,24},{24,16},{1,9},{9,1},{17,25},{25,17},{2,10},{10... | collective-permute-start | bytes 1966088 | tf_op jit(solution)/shard_map/ppermute | solution.py:61
  41.9 17.7 %copy-start.12 = (bf16[8,320,128]{2,1,0:T(8,128)(2,1)}, bf16[8,320,128]{2,1,0:T(8,128)(2,1)S(1)}, u32[]{:S(2)}) copy-start(bf16[8,320,128]{2,1,0:T(8,128)(2,1)S(1)} %pad_maximum_fusion.5.refs_8_) | copy-start | bytes 1966084
  41.9 17.3 %copy-start.39 = (s32[8,64,2]{1,2,0:T(2,128)S(1)}, s32[8,64,2]{1,2,0:T(2,128)}, u32[]{:S(2)}) copy-start(s32[8,64,2]{1,2,0:T(2,128)} %param.31) | copy-start | bytes 12292
  41.9 15.1 %collective-permute-start.9 = (bf16[8,320,128]{2,1,0:T(8,128)(2,1)S(1)}, bf16[8,320,128]{2,1,0:T(8,128)(2,1)}, u32[]{:S(2)}, u32[]{:S(2)}) collective-permute-start(bf16[8,320,128]{2,1,0:T(8,128)(2,1)S(1)} %pad_maximum_fusion.5.refs_8_), channel_id=1, source_target_pairs={{0,1},{1,0},{2,3},{3,2},{4,5},{5,4},{6,7},{7,6},{8,9},{9,8},{10,11... | collective-permute-start | bytes 1966088 | tf_op jit(solution)/shard_map/ppermute | solution.py:61
  44.0 15.6 %copy-start.41 = (s32[8,64]{1,0:T(8,128)S(1)}, s32[8,64]{1,0:T(8,128)}, u32[]{:S(2)}) copy-start(s32[8,64]{1,0:T(8,128)} %param.33) | copy-start | bytes 6148
  44.0 15.8 %copy-start.38 = (f32[8,64,2]{1,2,0:T(2,128)S(1)}, f32[8,64,2]{1,2,0:T(2,128)}, u32[]{:S(2)}) copy-start(f32[8,64,2]{1,2,0:T(2,128)} %param.32) | copy-start | bytes 12292
  44.9 23.6 %collective-permute-start.4 = (bf16[8,384,128]{2,1,0:T(8,128)(2,1)S(1)}, bf16[8,384,128]{2,1,0:T(8,128)(2,1)}, u32[]{:S(2)}, u32[]{:S(2)}) collective-permute-start(bf16[8,384,128]{2,1,0:T(8,128)(2,1)S(1)} %pad_maximum_fusion.4.refs_4_), channel_id=1, source_target_pairs={{0,8},{8,0},{16,24},{24,16},{1,9},{9,1},{17,25},{25,17},{2,10},{10... | collective-permute-start | bytes 2359304 | tf_op jit(solution)/shard_map/ppermute | solution.py:61
  53.1 15.4 %collective-permute-start.5 = (bf16[8,384,128]{2,1,0:T(8,128)(2,1)}, bf16[8,384,128]{2,1,0:T(8,128)(2,1)}, u32[]{:S(2)}, u32[]{:S(2)}) collective-permute-start(bf16[8,384,128]{2,1,0:T(8,128)(2,1)} %collective-permute-done.3.refs_5_), channel_id=1, source_target_pairs={{0,8},{8,0},{16,24},{24,16},{1,9},{9,1},{17,25},{25,17},{2,10},{10... | collective-permute-start | bytes 2359304 | tf_op jit(solution)/shard_map/ppermute | solution.py:61
  53.1 15.3 %collective-permute-start.10 = (bf16[8,320,128]{2,1,0:T(8,128)(2,1)S(1)}, bf16[8,320,128]{2,1,0:T(8,128)(2,1)}, u32[]{:S(2)}, u32[]{:S(2)}) collective-permute-start(bf16[8,320,128]{2,1,0:T(8,128)(2,1)S(1)} %pad_maximum_fusion.5.refs_8_), channel_id=1, source_target_pairs={{0,8},{8,0},{16,24},{24,16},{1,9},{9,1},{17,25},{25,17},{2,10},{10... | collective-permute-start | bytes 1966088 | tf_op jit(solution)/shard_map/ppermute | solution.py:61
  53.7 14.7 %collective-permute-start.17 = (bf16[8,320,128]{2,1,0:T(8,128)(2,1)}, bf16[8,320,128]{2,1,0:T(8,128)(2,1)}, u32[]{:S(2)}, u32[]{:S(2)}) collective-permute-start(bf16[8,320,128]{2,1,0:T(8,128)(2,1)} %collective-permute-done.15.refs_13_), channel_id=1, source_target_pairs={{0,8},{8,0},{16,24},{24,16},{1,9},{9,1},{17,25},{25,17},{2,10},{10... | collective-permute-start | bytes 1966088 | tf_op jit(solution)/shard_map/ppermute | solution.py:61
  57.0 11.4 %collective-permute-start.11 = (bf16[8,320,128]{2,1,0:T(8,128)(2,1)}, bf16[8,320,128]{2,1,0:T(8,128)(2,1)}, u32[]{:S(2)}, u32[]{:S(2)}) collective-permute-start(bf16[8,320,128]{2,1,0:T(8,128)(2,1)} %collective-permute-done.9.refs_9_), channel_id=1, source_target_pairs={{0,8},{8,0},{16,24},{24,16},{1,9},{9,1},{17,25},{25,17},{2,10},{10... | collective-permute-start | bytes 1966088 | tf_op jit(solution)/shard_map/ppermute | solution.py:61
  152.5 5.4 %collective-permute-start.28 = (bf16[16,368,128]{2,1,0:T(8,128)(2,1)}, bf16[16,368,128]{2,1,0:T(8,128)(2,1)}, u32[]{:S(2)}, u32[]{:S(2)}) collective-permute-start(bf16[16,368,128]{2,1,0:T(8,128)(2,1)} %get-tuple-element.34), channel_id=1, source_target_pairs={{0,8},{8,0},{16,24},{24,16},{1,9},{9,1},{17,25},{25,17},{2,10},{10... | collective-permute-start | bytes 4521992 | tf_op jit(solution)/shard_map/ppermute | solution.py:61
  153.1 8.7 %collective-permute-start.23 = (bf16[16,368,128]{2,1,0:T(8,128)(2,1)}, bf16[16,368,128]{2,1,0:T(8,128)(2,1)S(1)}, u32[]{:S(2)}, u32[]{:S(2)}) collective-permute-start(bf16[16,368,128]{2,1,0:T(8,128)(2,1)} %get-tuple-element.32), channel_id=1, source_target_pairs={{0,8},{8,0},{16,24},{24,16},{1,9},{9,1},{17,25},{25,17},{2,10},{10... | collective-permute-start | bytes 4521992 | tf_op jit(solution)/shard_map/ppermute | solution.py:61
  153.2 9.5 %collective-permute-start.18 = (bf16[16,384,128]{2,1,0:T(8,128)(2,1)}, bf16[16,384,128]{2,1,0:T(8,128)(2,1)S(1)}, u32[]{:S(2)}, u32[]{:S(2)}) collective-permute-start(bf16[16,384,128]{2,1,0:T(8,128)(2,1)} %get-tuple-element.30), channel_id=1, source_target_pairs={{0,8},{8,0},{16,24},{24,16},{1,9},{9,1},{17,25},{25,17},{2,10},{10... | collective-permute-start | bytes 4718600 | tf_op jit(solution)/shard_map/ppermute | solution.py:61
  159.9 19.1 %collective-permute-start.29 = (bf16[8,368,128]{2,1,0:T(8,128)(2,1)S(1)}, bf16[8,368,128]{2,1,0:T(8,128)(2,1)S(1)}, u32[]{:S(2)}, u32[]{:S(2)}) collective-permute-start(bf16[8,368,128]{2,1,0:T(8,128)(2,1)S(1)} %slice.534), channel_id=1, source_target_pairs={{0,2},{1,3},{2,0},{3,1},{4,6},{5,7},{6,4},{7,5},{8,10},{9,11},{10,... | collective-permute-start | bytes 2261000 | tf_op jit(solution)/shard_map/ppermute | solution.py:61
  162.3 18.6 %collective-permute-start.24 = (bf16[8,368,128]{2,1,0:T(8,128)(2,1)S(1)}, bf16[8,368,128]{2,1,0:T(8,128)(2,1)S(1)}, u32[]{:S(2)}, u32[]{:S(2)}) collective-permute-start(bf16[8,368,128]{2,1,0:T(8,128)(2,1)S(1)} %slice.535), channel_id=1, source_target_pairs={{0,1},{1,0},{2,3},{3,2},{4,5},{5,4},{6,7},{7,6},{8,9},{9,8},{10,11... | collective-permute-start | bytes 2261000 | tf_op jit(solution)/shard_map/ppermute | solution.py:61
  164.3 20.5 %collective-permute-start.19 = (bf16[8,384,128]{2,1,0:T(8,128)(2,1)S(1)}, bf16[8,384,128]{2,1,0:T(8,128)(2,1)S(1)}, u32[]{:S(2)}, u32[]{:S(2)}) collective-permute-start(bf16[8,384,128]{2,1,0:T(8,128)(2,1)S(1)} %slice.533), channel_id=1, source_target_pairs={{0,16},{8,24},{16,0},{24,8},{1,17},{9,25},{17,1},{25,9},{2,18},{10... | collective-permute-start | bytes 2359304 | tf_op jit(solution)/shard_map/ppermute | solution.py:61
  179.1 12.5 %collective-permute-start.30 = (bf16[4,368,128]{2,1,0:T(8,128)(2,1)S(1)}, bf16[4,368,128]{2,1,0:T(8,128)(2,1)S(1)}, u32[]{:S(2)}, u32[]{:S(2)}) collective-permute-start(bf16[4,368,128]{2,1,0:T(8,128)(2,1)S(1)} %slice.537), channel_id=1, source_target_pairs={{0,16},{8,24},{16,0},{24,8},{1,17},{9,25},{17,1},{25,9},{2,18},{10... | collective-permute-start | bytes 1130504 | tf_op jit(solution)/shard_map/ppermute | solution.py:61
  181.1 11.1 %collective-permute-start.25 = (bf16[4,368,128]{2,1,0:T(8,128)(2,1)S(1)}, bf16[4,368,128]{2,1,0:T(8,128)(2,1)S(1)}, u32[]{:S(2)}, u32[]{:S(2)}) collective-permute-start(bf16[4,368,128]{2,1,0:T(8,128)(2,1)S(1)} %slice.538), channel_id=1, source_target_pairs={{0,2},{1,3},{2,0},{3,1},{4,6},{5,7},{6,4},{7,5},{8,10},{9,11},{10,... | collective-permute-start | bytes 1130504 | tf_op jit(solution)/shard_map/ppermute | solution.py:61
  185.0 9.3 %collective-permute-start.20 = (bf16[4,384,128]{2,1,0:T(8,128)(2,1)S(1)}, bf16[4,384,128]{2,1,0:T(8,128)(2,1)S(1)}, u32[]{:S(2)}, u32[]{:S(2)}) collective-permute-start(bf16[4,384,128]{2,1,0:T(8,128)(2,1)S(1)} %slice.536), channel_id=1, source_target_pairs={{0,1},{1,0},{2,3},{3,2},{4,5},{5,4},{6,7},{7,6},{8,9},{9,8},{10,11... | collective-permute-start | bytes 1179656 | tf_op jit(solution)/shard_map/ppermute | solution.py:61
  191.8 10.2 %collective-permute-start.31 = (f32[2,368,128]{2,1,0:T(8,128)S(1)}, f32[2,368,128]{2,1,0:T(8,128)S(1)}, u32[]{:S(2)}, u32[]{:S(2)}) collective-permute-start(f32[2,368,128]{2,1,0:T(8,128)S(1)} %slice.423), channel_id=1, source_target_pairs={{0,1},{1,0},{2,3},{3,2},{4,5},{5,4},{6,7},{7,6},{8,9},{9,8},{10,11... | collective-permute-start | bytes 1130504 | tf_op jit(solution)/shard_map/ppermute | solution.py:61
  192.3 20.5 %collective-permute-start.26 = (f32[2,368,128]{2,1,0:T(8,128)S(1)}, f32[2,368,128]{2,1,0:T(8,128)S(1)}, u32[]{:S(2)}, u32[]{:S(2)}) collective-permute-start(f32[2,368,128]{2,1,0:T(8,128)S(1)} %slice.415), channel_id=1, source_target_pairs={{0,4},{1,5},{2,6},{3,7},{4,0},{5,1},{6,2},{7,3},{8,12},{9,13},{10,... | collective-permute-start | bytes 1130504 | tf_op jit(solution)/shard_map/ppermute | solution.py:61
  194.5 19.4 %collective-permute-start.21 = (f32[2,384,128]{2,1,0:T(8,128)S(1)}, f32[2,384,128]{2,1,0:T(8,128)S(1)}, u32[]{:S(2)}, u32[]{:S(2)}) collective-permute-start(f32[2,384,128]{2,1,0:T(8,128)S(1)} %slice.407), channel_id=1, source_target_pairs={{0,2},{1,3},{2,0},{3,1},{4,6},{5,7},{6,4},{7,5},{8,10},{9,11},{10,... | collective-permute-start | bytes 1179656 | tf_op jit(solution)/shard_map/ppermute | solution.py:61
  202.0 21.3 %collective-permute-start.32 = (f32[1,368,128]{2,1,0:T(8,128)S(1)}, f32[1,368,128]{2,1,0:T(8,128)S(1)}, u32[]{:S(2)}, u32[]{:S(2)}) collective-permute-start(f32[1,368,128]{2,1,0:T(8,128)S(1)} %slice.425), channel_id=1, source_target_pairs={{0,4},{1,5},{2,6},{3,7},{4,0},{5,1},{6,2},{7,3},{8,12},{9,13},{10,... | collective-permute-start | bytes 565256 | tf_op jit(solution)/shard_map/ppermute | solution.py:61
  212.9 11.1 %collective-permute-start.27 = (f32[1,368,128]{2,1,0:T(8,128)S(1)}, f32[1,368,128]{2,1,0:T(8,128)S(1)}, u32[]{:S(2)}, u32[]{:S(2)}) collective-permute-start(f32[1,368,128]{2,1,0:T(8,128)S(1)} %slice.417), channel_id=1, source_target_pairs={{0,16},{8,24},{16,0},{24,8},{1,17},{9,25},{17,1},{25,9},{2,18},{10... | collective-permute-start | bytes 565256 | tf_op jit(solution)/shard_map/ppermute | solution.py:61
  213.9 16.5 %collective-permute-start.22 = (f32[1,384,128]{2,1,0:T(8,128)S(1)}, f32[1,384,128]{2,1,0:T(8,128)S(1)}, u32[]{:S(2)}, u32[]{:S(2)}) collective-permute-start(f32[1,384,128]{2,1,0:T(8,128)S(1)} %slice.409), channel_id=1, source_target_pairs={{0,4},{1,5},{2,6},{3,7},{4,0},{5,1},{6,2},{7,3},{8,12},{9,13},{10,... | collective-permute-start | bytes 589832 | tf_op jit(solution)/shard_map/ppermute | solution.py:61
  224.7 5.0 %collective-permute-start.40 = (f32[1,96,128]{2,1,0:T(8,128)S(1)}, f32[1,96,128]{2,1,0:T(8,128)S(1)}, u32[]{:S(2)}, u32[]{:S(2)}) collective-permute-start(f32[1,96,128]{2,1,0:T(8,128)S(1)} %maximum_bitcast_fusion.3), channel_id=1, source_target_pairs={{0,4},{1,5},{2,6},{3,7},{4,0},{5,1},{6,2},{7,3},{8,12},{9,13},{10,... | collective-permute-start | bytes 147464 | tf_op jit(solution)/shard_map/ppermute | solution.py:61
  229.7 4.7 %collective-permute-start.41 = (f32[2,96,128]{2,1,0:T(8,128)S(1)}, f32[2,96,128]{2,1,0:T(8,128)S(1)}, u32[]{:S(2)}, u32[]{:S(2)}) collective-permute-start(f32[2,96,128]{2,1,0:T(8,128)S(1)} %pad_maximum_fusion.15), channel_id=1, source_target_pairs={{0,2},{1,3},{2,0},{3,1},{4,6},{5,7},{6,4},{7,5},{8,10},{9,11},{10,... | collective-permute-start | bytes 294920 | tf_op jit(solution)/shard_map/ppermute | solution.py:61
  234.4 5.7 %collective-permute-start.42 = (f32[4,96,128]{2,1,0:T(8,128)S(1)}, f32[4,96,128]{2,1,0:T(8,128)S(1)}, u32[]{:S(2)}, u32[]{:S(2)}) collective-permute-start(f32[4,96,128]{2,1,0:T(8,128)S(1)} %pad_maximum_fusion.12), channel_id=1, source_target_pairs={{0,1},{1,0},{2,3},{3,2},{4,5},{5,4},{6,7},{7,6},{8,9},{9,8},{10,11... | collective-permute-start | bytes 589832 | tf_op jit(solution)/shard_map/ppermute | solution.py:61
  240.1 7.8 %collective-permute-start.43 = (f32[8,96,128]{2,1,0:T(8,128)S(1)}, f32[8,96,128]{2,1,0:T(8,128)S(1)}, u32[]{:S(2)}, u32[]{:S(2)}) collective-permute-start(f32[8,96,128]{2,1,0:T(8,128)S(1)} %pad_maximum_fusion.8), channel_id=1, source_target_pairs={{0,16},{8,24},{16,0},{24,8},{1,17},{9,25},{17,1},{25,9},{2,18},{10... | collective-permute-start | bytes 1179656 | tf_op jit(solution)/shard_map/ppermute | solution.py:61
  248.9 31.8 %collective-permute-start.44 = (f32[16,96,128]{2,1,0:T(8,128)}, f32[16,96,128]{2,1,0:T(8,128)S(1)}, u32[]{:S(2)}, u32[]{:S(2)}) collective-permute-start(f32[16,96,128]{2,1,0:T(8,128)} %get-tuple-element.64), channel_id=1, source_target_pairs={{0,8},{8,0},{16,24},{24,16},{1,9},{9,1},{17,25},{25,17},{2,10},{10... | collective-permute-start | bytes 2359304 | tf_op jit(solution)/shard_map/ppermute | solution.py:61
  248.9 30.7 %collective-permute-start.38 = (f32[1,1024,128]{2,1,0:T(8,128)S(1)}, f32[1,1024,128]{2,1,0:T(8,128)S(1)}, u32[]{:S(2)}, u32[]{:S(2)}) collective-permute-start(f32[1,1024,128]{2,1,0:T(8,128)S(1)} %bitcast.126), channel_id=1, source_target_pairs={{0,16},{8,24},{16,0},{24,8},{1,17},{9,25},{17,1},{25,9},{2,18},{10... | collective-permute-start | bytes 1572872 | tf_op jit(solution)/shard_map/ppermute | solution.py:61
  253.2 1.2 collective-permute-start.33
  254.5 8.9 %collective-permute-start.34 = (f32[3]{0:T(128)S(1)}, f32[3]{0:T(128)S(1)}, u32[]{:S(2)}, u32[]{:S(2)}) collective-permute-start(f32[3]{0:T(128)S(1)} %fusion.84), channel_id=1, source_target_pairs={{0,16},{8,24},{16,0},{24,8},{1,17},{9,25},{17,1},{25,9},{2,18},{10... | collective-permute-start | bytes 44 | tf_op jit(solution)/shard_map/ppermute | solution.py:61
  263.4 3.6 collective-permute-start.35
  266.9 3.6 collective-permute-start.36
  270.5 4.5 %collective-permute-start.37 = (f32[3]{0:T(128)S(1)}, f32[3]{0:T(128)S(1)}, u32[]{:S(2)}, u32[]{:S(2)}) collective-permute-start(f32[3]{0:T(128)S(1)} %add.744), channel_id=1, source_target_pairs={{0,4},{1,5},{2,6},{3,7},{4,0},{5,1},{6,2},{7,3},{8,12},{9,13},{10,... | collective-permute-start | bytes 44 | tf_op jit(solution)/shard_map/ppermute | solution.py:61
  280.7 9.3 %collective-permute-start.39 = (f32[2,1024,128]{2,1,0:T(8,128)}, f32[2,1024,128]{2,1,0:T(8,128)}, u32[]{:S(2)}, u32[]{:S(2)}) collective-permute-start(f32[2,1024,128]{2,1,0:T(8,128)} %pad_maximum_fusion.3), channel_id=1, source_target_pairs={{0,8},{8,0},{16,24},{24,16},{1,9},{9,1},{17,25},{25,17},{2,10},{10... | collective-permute-start | bytes 3145736 | tf_op jit(solution)/shard_map/ppermute | solution.py:61
  362.4 4.6 %copy-start.25 = (f32[256,512]{1,0:T(8,128)S(1)}, f32[256,512]{1,0:T(8,128)}, u32[]{:S(2)}) copy-start(f32[256,512]{1,0:T(8,128)} %param.42) | copy-start | bytes 1572868
  362.4 4.6 %copy-start.28 = (f32[256,512]{1,0:T(8,128)S(1)}, f32[256,512]{1,0:T(8,128)}, u32[]{:S(2)}) copy-start(f32[256,512]{1,0:T(8,128)} %param.43) | copy-start | bytes 1572868
  362.4 4.6 %copy-start.29 = (f32[256,512]{1,0:T(8,128)S(1)}, f32[256,512]{1,0:T(8,128)}, u32[]{:S(2)}) copy-start(f32[256,512]{1,0:T(8,128)} %param.44) | copy-start | bytes 1572868
  (26 other events, 69.7 us)
where the time goes:
time: 377 us; the launch traced here: 371 us
  Pallas kernels  127 us (34%)
  waiting for transfers between devices  110 us (29%)
  starting transfers between devices  36.3 us (10%)
  other arithmetic  35 us (9%)
  local copies, waits for them, and re-layouts  32.8 us (9%)
  matrix products  20.1 us (5%)
  between operations  10.3 us (3%)
    ppermute x45, waiting for transfers between devices, swap(): return lax.ppermute(value, axis, [(i, i ^ bit) for i in range(size)])  110 us
    pallas_call x1, Pallas kernels, model_grads(): pl.pallas_call(functools.partial(model_kernel, fast, PART_ROWS), out_shap...  82.8 us
    pallas_call x1, Pallas kernels, renew_all(): pl.pallas_call(functools.partial(qr_kernel, count), out_shape=jax.ShapeDt...  43.9 us
    ppermute x45, starting transfers between devices, swap(): return lax.ppermute(value, axis, [(i, i ^ bit) for i in range(size)])  36.3 us
  transfers between devices with their start and end apart: 45, of which 24 were waited for; matrix products, arithmetic and copies ran while one was open for 13% of the time, Pallas kernels for 0%

commit v1 on v0

--- a/solution.py
+++ b/solution.py
@@ -61,13 +61,6 @@
     return lax.ppermute(value, axis, [(i, i ^ bit) for i in range(size)])
 
 
-def sum_small(value, dp, fsdp):
-    for axis, size in (("dp", dp), ("fsdp", fsdp)):
-        for bit in reversed(halves(size)):
-            value = value + swap(value, axis, size, bit)
-    return value
-
-
 def part_orders(dp, fsdp):
     core, tall = [("dp", dp, bit) for bit in reversed(halves(dp))]
     deep, near, side = [("fsdp", fsdp, bit) for bit in halves(fsdp)]
@@ -133,7 +126,7 @@
     return jnp.stack(units), jnp.stack(spots)
 
 
-def gathered_pieces(blocks_low, maps_low, dp, fsdp):
+def gathered_pieces(blocks_low, maps_low, ready, dp, fsdp):
     dp_here = lax.axis_index("dp")
     quarter = blocks_low.shape[0] // dp
     piece_rows = maps_low.shape[0] // dp
@@ -147,9 +140,13 @@
             0,
         )
         held = gather_doubling(piece, order[2:])
-        both = [held, swap(held, *order[1])]
-        pieces += both + [swap(piece, *order[0]) for piece in both]
-    return pieces
+        pieces.append([held, swap(held, *order[1])])
+    pieces[-1][1], ready = lax.optimization_barrier((pieces[-1][1], ready))
+    return [
+        piece
+        for both, order in zip(pieces, part_orders(dp, fsdp))
+        for piece in both + [swap(piece, *order[0]) for piece in both]
+    ], ready
 
 
 def reduced_grads(outs, sums, slots, map_rows, dp, fsdp):
@@ -176,7 +173,9 @@
     own_maps = jnp.concatenate([parts[0][cut:], parts[1][cut : cut + 64], parts[2][cut : cut + 64]], 0)
     own_heads = jnp.concatenate([parts[1][cut + 64 :], parts[2][cut + 64 :]], 0)
     own_square = sum(jnp.sum(part * part) for part in parts)
-    sums = sum_small(jnp.concatenate([sums, own_square[None]]), dp, fsdp)
+    totals = jnp.concatenate([sums, own_square[None]])
+    totals = jnp.pad(totals[None], ((0, 7), (0, BS - totals.shape[0])))
+    own_heads = jnp.concatenate([own_heads, totals], 0)
     dp_order = [("dp", dp, bit) for bit in reversed(halves(dp))]
     spot = inverse_place(dp_order, dp, 1, dp_here, 0).reshape(-1)
     shard = gather_doubling(jnp.concatenate([own_blocks, own_maps], 0), dp_order)
@@ -190,10 +189,13 @@
         .transpose(0, 2, 1, 3)
         .reshape(map_rows, D)
     )
-    full_order = part_orders(dp, fsdp)[0]
+    core, tall, side, near, deep = part_orders(dp, fsdp)[0]
+    full_order = (core, deep, side, near, tall)
     all_heads = gather_doubling(own_heads, full_order)
     spot = inverse_place(full_order, dp, fsdp, dp_here, fsdp_here).reshape(-1)
-    return block_grad, maps_grad, all_heads[spot].reshape(-1, BS), sums[-1], sums[:-1]
+    all_heads = all_heads[spot]
+    sums = jnp.sum(all_heads[:, -8, :3], 0)
+    return block_grad, maps_grad, all_heads[:, :-8].reshape(-1, BS), sums[-1], sums[:-1]
 
 
 def norm_rows(inputs, gain_row, bias_row):
@@ -630,9 +632,9 @@
     tokens = seqs_here * F
     blocks_low = blocks.astype(jnp.bfloat16)
     maps_low = latent_maps.astype(jnp.bfloat16)
-    inverse = jnp.argsort(owner_order).astype(jnp.int32)
+    slot_ids = jnp.arange(owner_order.shape[0], dtype=jnp.int32)
+    inverse = jnp.sum(jnp.where(owner_order[None, :] == slot_ids[:, None], slot_ids[None, :], 0), 1)
     if fast:
-        sources = gathered_pieces(blocks_low, maps_low, dp, fsdp)
         units, spots = placed_units(dp, fsdp)
         part_ids = jnp.arange(3)[:, None]
         unit_place = (part_ids << 8) + spots
@@ -736,6 +738,14 @@
         pltpu.SemaphoreType.DMA,
         pltpu.SemaphoreType.DMA((6,)),
     ]
+    inputs = (
+        owner_order, units, block_place, unit_place,
+        one_hot_rows(latents), one_hot_rows(jnp.roll(latents, -1, axis=1)),
+        jnp.broadcast_to(later[None], (8, tokens)), base, facts, legal, next_hot, act_hot, gains,
+        head_wide, jnp.broadcast_to(head_bias, (8, HEAD_COLS)),
+    )
+    if fast:
+        sources, inputs = gathered_pieces(blocks_low, maps_low, inputs, dp, fsdp)
     *outs, sums = pl.pallas_call(
         functools.partial(model_kernel, fast, PART_ROWS),
         out_shape=[jax.ShapeDtypeStruct(shape, kind) for shape, kind in shapes],
@@ -744,12 +754,7 @@
         scratch_shapes=scratch,
         compiler_params=pltpu.CompilerParams(vmem_limit_bytes=66 * 1000 * 1000),
         name="model",
-    )(
-        owner_order, units, block_place, unit_place, *sources,
-        one_hot_rows(latents), one_hot_rows(jnp.roll(latents, -1, axis=1)),
-        jnp.broadcast_to(later[None], (8, tokens)), base, facts, legal, next_hot, act_hot, gains,
-        head_wide, jnp.broadcast_to(head_bias, (8, HEAD_COLS)),
-    )
+    )(*inputs[:4], *sources, *inputs[4:])
     return reduced_grads(outs, sums[:2, 0], blocks.shape[0], latent_maps.shape[0], dp, fsdp)
 
 
@@ -877,7 +882,7 @@
     )(stats, bases)
 
 
-def soap_update(weight, first_moment, second_moment, left, right, left_rot, right_rot, grad):
+def soap_update(weight, first_moment, second_moment, left, right, left_rot, right_rot, grad, dp):
     left = beta_two * left + (1.0 - beta_two) * jnp.einsum(
         "bij,bkj->bik", grad, grad, precision=HIGHEST
     )
@@ -896,18 +901,17 @@
     direction = jnp.einsum("bij,bjk->bik", left_rot, direction, precision=HIGHEST)
     direction = jnp.einsum("bij,bkj->bik", direction, right_rot, precision=HIGHEST)
     weight = weight - learn_rate * (direction + weight_decay * weight)
-    count = weight.shape[0]
-    renewed = renew_all(
-        jnp.concatenate([left, right], 0), jnp.concatenate([left_rot, right_rot], 0)
-    )
+    is_left = lax.axis_index("dp") % 2 == 0
+    renewed = renew_all(jnp.where(is_left, left, right), jnp.where(is_left, left_rot, right_rot))
+    other = swap(renewed, "dp", dp, 1)
     return (
         weight,
         first_moment,
         second_moment,
         left,
         right,
-        renewed[:count],
-        renewed[count:],
+        jnp.where(is_left, renewed, other),
+        jnp.where(is_left, other, renewed),
     )
 
 
@@ -970,6 +974,7 @@
         left_basis,
         right_basis,
         block_grad * factor,
+        dp,
     )
     maps_out = adam_update(
         latent_maps, latent_first, latent_second, maps_grad * factor, weight_decay, learn_rate

time: 377 us -> 373 us (0.989)
  waiting for transfers between devices: 110 us -> 93.1 us
  Pallas kernels: 127 us -> 111 us
  local copies, waits for them, and re-layouts: 32.8 us -> 48 us
  starting transfers between devices: 36.3 us -> 45.8 us
    ppermute x45 -> x41, waiting for transfers between devices: 110 us -> 93.1 us  [swap(): return lax.ppermute(value, axis, [(i, i ^ bit) for i in range(size)])]
    pallas_call x1, Pallas kernels: 43.9 us -> 28.4 us  [renew_all(): pl.pallas_call(functools.partial(qr_kernel, count), out_shape=jax.ShapeDt...]
    unnamed x108 -> x132, local copies, waits for them, and re-layouts: 6.25 us -> 19.3 us
    ppermute x45 -> x41, starting transfers between devices: 36.3 us -> 45.8 us  [swap(): return lax.ppermute(value, axis, [(i, i ^ bit) for i in range(size)])]
    concatenate x14, other arithmetic: 2.83 us -> 9.13 us  [gather_doubling(): held = jnp.concatenate([held, swap(held, axis, size, bit)], 0)]
    concatenate x3 -> x0, other arithmetic: 6.23 us -> none  [the longest x1 4.16 us: soap_update(): jnp.concatenate([left_rot, right_rot], 0)]
    select_n x1 -> x3, other arithmetic: 0.01 us -> 4.69 us  [the longest x1 3.37 us: soap_update(): jnp.where(is_left, other, renewed)]
    slice x1, local copies, waits for them, and re-layouts: 4.04 us -> 0.18 us  [reduced_grads(): all_heads[:, :-8].reshape(-1, BS)]
  transfers between devices with their start and end apart: 45 -> 41, of which waited for: 24 -> 21; matrix products, arithmetic and copies ran while one was open for 13% -> 18% of each run, Pallas kernels for 0% -> 0%
where the time goes in v1:
time: 373 us; the launch traced here: 369 us
  Pallas kernels  111 us (30%)
  waiting for transfers between devices  93.1 us (25%)
  local copies, waits for them, and re-layouts  48 us (13%)
  starting transfers between devices  45.8 us (12%)
  other arithmetic  38 us (10%)
  matrix products  22.9 us (6%)
  between operations  10.2 us (3%)
    ppermute x41, waiting for transfers between devices, swap(): return lax.ppermute(value, axis, [(i, i ^ bit) for i in range(size)])  93.1 us
    pallas_call x1, Pallas kernels, model_grads(): pl.pallas_call(functools.partial(model_kernel, fast, PART_ROWS), out_shap...  82.7 us
    ppermute x41, starting transfers between devices, swap(): return lax.ppermute(value, axis, [(i, i ^ bit) for i in range(size)])  45.8 us
    pallas_call x1, Pallas kernels, renew_all(): pl.pallas_call(functools.partial(qr_kernel, count), out_shape=jax.ShapeDt...  28.4 us
    unnamed x132, local copies, waits for them, and re-layouts  19.3 us
    concatenate x14, other arithmetic, gather_doubling(): held = jnp.concatenate([held, swap(held, axis, size, bit)], 0)  9.13 us
  transfers between devices with their start and end apart: 41, of which 21 were waited for; matrix products, arithmetic and copies ran while one was open for 18% of the time, Pallas kernels for 0%

profile of v1, /device:TPU:0, one launch (start us, length us, event | category | flops | bytes accessed | tf_op | source)
XLA Modules:
  0.0 369.1 jit_solution(9460304305813031440)
XLA Ops:
  0.7 1.1 dynamic-slice_convert_fusion
  2.8 4.1 %collective-permute-start.4 = (bf16[1,384,128]{2,1,0:T(8,128)(2,1)S(1)}, bf16[1,384,128]{2,1,0:T(8,128)(2,1)S(1)}, u32[]{:S(2)}, u32[]{:S(2)}) collective-permute-start(bf16[1,384,128]{2,1,0:T(8,128)(2,1)S(1)} %maximum_bitcast_fusion), channel_id=1, source_target_pairs={{0,4},{1,5},{2,6},{3,7},{4,0},{5,1},{6,2},{7,3},{8,12},{9,13},{10,... | collective-permute-start | bytes 294920 | tf_op jit(solution)/shard_map/ppermute | solution.py:61
  7.1 1.8 collective-permute-start.10
  13.7 1.2 fusion.20
  15.1 1.6 collective-permute-start.5
  16.8 2.7 collective-permute-start.11
  19.4 4.8 %collective-permute-done.5 = bf16[2,384,128]{2,1,0:T(8,128)(2,1)S(1)} collective-permute-done((bf16[2,384,128]{2,1,0:T(8,128)(2,1)S(1)}, bf16[2,384,128]{2,1,0:T(8,128)(2,1)S(1)}, u32[]{:S(2)}, u32[]{:S(2)}) %collective-permute-start.5) | collective-permute-done | bytes 196640 | tf_op jit(solution)/shard_map/ppermute | solution.py:61
  24.3 1.6 collective-permute-start.6
  27.8 6.0 %collective-permute-done.1 = bf16[2,320,128]{2,1,0:T(8,128)(2,1)S(1)} collective-permute-done((bf16[2,320,128]{2,1,0:T(8,128)(2,1)S(1)}, bf16[2,320,128]{2,1,0:T(8,128)(2,1)S(1)}, u32[]{:S(2)}, u32[]{:S(2)}) %collective-permute-start.1) | collective-permute-done | bytes 163872 | tf_op jit(solution)/shard_map/ppermute | solution.py:61
  34.7 1.1 collective-permute-start.2
  39.8 1.7 gather_fusion
  42.4 1.7 fusion.1
  44.2 2.0 concatenate.131.refs_25_
  46.4 1.1 concatenate.129.refs_20_
  48.6 1.6 collective-permute-start.13
  51.2 1.6 collective-permute-start.3
  53.0 1.6 convolution_add_fusion.refs_19_
  55.9 12.6 %collective-permute-done.3.refs_13_ = bf16[8,320,128]{2,1,0:T(8,128)(2,1)S(1)} collective-permute-done((bf16[8,320,128]{2,1,0:T(8,128)(2,1)S(1)}, bf16[8,320,128]{2,1,0:T(8,128)(2,1)S(1)}, u32[]{:S(2)}, u32[]{:S(2)}) %collective-permute-start.3) | collective-permute-done | bytes 655392 | tf_op jit(solution)/shard_map/ppermute | solution.py:61
  73.7 82.7 %model.1 = (f32[16,384,128]{2,1,0:T(8,128)}, bf16[16,384,128]{2,1,0:T(8,128)(2,1)}, f32[16,368,128]{2,1,0:T(8,128)}, bf16[16,368,128]{2,1,0:T(8,128)(2,1)}, f32[...) custom-call(s32[192]{0:T(256)} %refs_0_, s32[96]{0:T(128)} %reshape.1024.refs_1_, ...), custom_call_target="tpu_custom_call" | custom-call | tf_op jit(solution)/shard_map/model/pallas_call | solution.py:749
  157.4 2.6 collective-permute-done.23
  160.1 2.3 convert_add_fusion.1
  162.5 1.6 collective-permute-start.24
  167.9 13.8 %collective-permute-done.24 = bf16[8,368,128]{2,1,0:T(8,128)(2,1)S(1)} collective-permute-done((bf16[8,368,128]{2,1,0:T(8,128)(2,1)S(1)}, bf16[8,368,128]{2,1,0:T(8,128)(2,1)S(1)}, u32[]{:S(2)}, u32[]{:S(2)}) %collective-permute-start.24) | collective-permute-done | bytes 753696 | tf_op jit(solution)/shard_map/ppermute | solution.py:61
  181.9 1.1 collective-permute-start.25
  184.3 2.7 collective-permute-done.29
  187.8 6.3 %collective-permute-done.25 = bf16[4,368,128]{2,1,0:T(8,128)(2,1)S(1)} collective-permute-done((bf16[4,368,128]{2,1,0:T(8,128)(2,1)S(1)}, bf16[4,368,128]{2,1,0:T(8,128)(2,1)S(1)}, u32[]{:S(2)}, u32[]{:S(2)}) %collective-permute-start.25) | collective-permute-done | bytes 376864 | tf_op jit(solution)/shard_map/ppermute | solution.py:61
  194.9 5.9 %collective-permute-start.21 = (f32[2,368,128]{2,1,0:T(8,128)S(1)}, f32[2,368,128]{2,1,0:T(8,128)S(1)}, u32[]{:S(2)}, u32[]{:S(2)}) collective-permute-start(f32[2,368,128]{2,1,0:T(8,128)S(1)} %slice.407), channel_id=1, source_target_pairs={{0,4},{1,5},{2,6},{3,7},{4,0},{5,1},{6,2},{7,3},{8,12},{9,13},{10,... | collective-permute-start | bytes 1130504 | tf_op jit(solution)/shard_map/ppermute | solution.py:61
  201.6 3.1 collective-permute-done.26
  204.7 6.0 %collective-permute-start.27 = (f32[1,368,128]{2,1,0:T(8,128)S(1)}, f32[1,368,128]{2,1,0:T(8,128)S(1)}, u32[]{:S(2)}, u32[]{:S(2)}) collective-permute-start(f32[1,368,128]{2,1,0:T(8,128)S(1)} %slice.418), channel_id=1, source_target_pairs={{0,4},{1,5},{2,6},{3,7},{4,0},{5,1},{6,2},{7,3},{8,12},{9,13},{10,... | collective-permute-start | bytes 565256 | tf_op jit(solution)/shard_map/ppermute | solution.py:61
  210.7 7.7 %collective-permute-done.21 = f32[2,368,128]{2,1,0:T(8,128)S(1)} collective-permute-done((f32[2,368,128]{2,1,0:T(8,128)S(1)}, f32[2,368,128]{2,1,0:T(8,128)S(1)}, u32[]{:S(2)}, u32[]{:S(2)}) %collective-permute-start.21) | collective-permute-done | bytes 376864 | tf_op jit(solution)/shard_map/ppermute | solution.py:61
  218.4 1.2 collective-permute-start.22
  219.7 9.7 %collective-permute-done.27 = f32[1,368,128]{2,1,0:T(8,128)S(1)} collective-permute-done((f32[1,368,128]{2,1,0:T(8,128)S(1)}, f32[1,368,128]{2,1,0:T(8,128)S(1)}, u32[]{:S(2)}, u32[]{:S(2)}) %collective-permute-start.27) | collective-permute-done | bytes 188448 | tf_op jit(solution)/shard_map/ppermute | solution.py:61
  230.7 2.6 collective-permute-done.32
  235.9 1.2 collective-permute-start.33
  240.9 4.0 %collective-permute-done.34 = f32[2,104,128]{2,1,0:T(8,128)S(1)} collective-permute-done((f32[2,104,128]{2,1,0:T(8,128)S(1)}, f32[2,104,128]{2,1,0:T(8,128)S(1)}, u32[]{:S(2)}, u32[]{:S(2)}) %collective-permute-start.34) | collective-permute-done | bytes 106528 | tf_op jit(solution)/shard_map/ppermute | solution.py:61
  244.9 1.7 collective-permute-start.35
  248.9 1.9 collective-permute-done.35
  250.8 1.5 collective-permute-start.36
  253.7 5.3 %collective-permute-done.38 = f32[1,1024,128]{2,1,0:T(8,128)} collective-permute-done((f32[1,1024,128]{2,1,0:T(8,128)}, f32[1,1024,128]{2,1,0:T(8,128)}, u32[]{:S(2)}, u32[]{:S(2)}) %collective-permute-start.38) | collective-permute-done | bytes 524320 | tf_op jit(solution)/shard_map/ppermute | solution.py:61
  259.0 2.2 pad_maximum_fusion.1
  262.0 7.3 %collective-permute-done.36 = f32[8,104,128]{2,1,0:T(8,128)S(1)} collective-permute-done((f32[8,104,128]{2,1,0:T(8,128)S(1)}, f32[8,104,128]{2,1,0:T(8,128)S(1)}, u32[]{:S(2)}, u32[]{:S(2)}) %collective-permute-start.36) | collective-permute-done | bytes 426016 | tf_op jit(solution)/shard_map/ppermute | solution.py:61
  270.4 1.3 broadcast_select_fusion.2.basis_ref
  271.7 3.0 pad_maximum_fusion
  274.7 3.6 gather_fusion.2
  278.3 2.1 constant_dynamic-update-slice_fusion.5
  280.4 2.1 gather_fusion.1
  286.6 1.9 slice_multiply_fusion.2
  288.4 1.5 slice_multiply_fusion
  290.7 1.8 slice_dynamic-update-slice_fusion.3
  292.5 1.7 slice_dynamic-update-slice_fusion.2
  294.2 1.7 slice_dynamic-update-slice_fusion.1
  295.8 1.7 slice_dynamic-update-slice_fusion
  300.3 1.1 copy.70
  301.4 3.9 %fusion.72 = f32[24,128,128]{1,2,0:T(8,128)} fusion(f32[24,128,128]{2,1,0:T(8,128)S(1)} %bitcast.116, f32[24,128,128]{2,1,0:T(8,128)S(1)} %copy-done.4), kind=kOutput, calls=%fused_computation.273 | convolution fusion | flops 603979776 | bytes 4718592 | tf_op jit(solution)/shard_map/bji,bjk->bik/dot_general | solution.py:892
  305.3 2.7 multiply_add_fusion
  308.1 5.3 %broadcast_select_fusion.3 = (f32[24,128,128]{2,1,0:T(8,128)}, f32[24,128,128]{2,1,0:T(8,128)}) fusion(f32[24,128,128]{2,1,0:T(8,128)S(1)} %multiply_add_fusion, pred[]{:T(512)S(6)} %eq.176, f32[24,128,128]{2,1,0:T(8,128)S(1)} %bitcast.118, f32[24,128,128]{2,1,0:T(8,128)S(1)} %copy-done.21), kind=kOutput, calls=%fused_computation.54 | convolution fusion | flops 605552640 | bytes 7864321 | tf_op jit(solution)/shard_map/bij,bkj->bik/dot_general | solution.py:886
  313.4 28.4 %renew.1 = f32[24,128,128]{2,1,0:T(8,128)} custom-call(f32[24,128,128]{2,1,0:T(8,128)} %get-tuple-element.125.stat_ref, f32[24,128,128]{2,1,0:T(8,128)} %broadcast_select_fusion.2.basis_ref), custom_call_target="tpu_custom_call" | custom-call | tf_op jit(solution)/shard_map/renew/pallas_call | solution.py:875
  343.8 1.2 copy-done.11
  345.0 4.6 %multiply_subtract_fusion.1 = (f32[513,529]{1,0:T(8,128)S(1)}, f32[513,529]{1,0:T(8,128)}, f32[513,529]{1,0:T(8,128)}) fusion(f32[513,529]{1,0:T(8,128)S(1)} %copy-done.11, f32[]{:T(128)S(6)} %div.195, f32[1,640]{1,0:T(1,128)S(1)} %constant_dynamic-update-slice_fusion.13, f32[512,640]{1,0:T(8,128)S(1)} %copy-done.2, f32[513,255]{1,0:T(8,128)S(1)} %get-tuple-element.91, ...), kind=kLoop, calls=%fused_computation.39 | loop fusion | flops 5970294 | bytes 8872852 | tf_op jit(solution)/shard_map/sub | solution.py:926
  351.5 1.4 multiply_subtract_fusion.2
  354.0 2.1 multiply_add_fusion.2
  356.2 2.5 fusion.3
  358.7 4.5 %multiply_subtract_fusion = f32[24,128,128]{2,1,0:T(8,128)} fusion(f32[24,128,128]{2,1,0:T(8,128)S(1)} %copy-done.20, f32[24,128,128]{1,2,0:T(8,128)S(1)} %fusion.3, f32[24,128,128]{2,1,0:T(8,128)S(1)} %copy-done.1), kind=kOutput, calls=%fused_computation.21 | convolution fusion | flops 605552640 | bytes 6291456 | tf_op jit(solution)/shard_map/bij,bkj->bik/dot_general | solution.py:902
  363.3 3.4 broadcast_select_fusion
  (315 shorter events, 51.1 us)
Async XLA Ops:
  0.7 8.3 %copy-start.52 = (s32[192]{0:T(256)S(1)}, s32[192]{0:T(256)}, u32[]{:S(2)}) copy-start(s32[192]{0:T(256)} %refs_0_) | copy-start | bytes 2308
  0.7 8.4 %copy-start.10 = (f32[513,529]{1,0:T(8,128)S(1)}, f32[513,529]{1,0:T(8,128)}, u32[]{:S(2)}) copy-start(f32[513,529]{1,0:T(8,128)} %param.45) | copy-start | bytes 3256528
  1.8 7.6 %copy-start.48 = (s32[8,64]{1,0:T(8,128)S(1)}, s32[8,64]{1,0:T(8,128)}, u32[]{:S(2)}) copy-start(s32[8,64]{1,0:T(8,128)} %param.27) | copy-start | bytes 6148
  2.8 12.2 %collective-permute-start.4 = (bf16[1,384,128]{2,1,0:T(8,128)(2,1)S(1)}, bf16[1,384,128]{2,1,0:T(8,128)(2,1)S(1)}, u32[]{:S(2)}, u32[]{:S(2)}) collective-permute-start(bf16[1,384,128]{2,1,0:T(8,128)(2,1)S(1)} %maximum_bitcast_fusion), channel_id=1, source_target_pairs={{0,4},{1,5},{2,6},{3,7},{4,0},{5,1},{6,2},{7,3},{8,12},{9,13},{10,... | collective-permute-start | bytes 294920 | tf_op jit(solution)/shard_map/ppermute | solution.py:61
  7.0 18.9 %collective-permute-start = (bf16[1,320,128]{2,1,0:T(8,128)(2,1)S(1)}, bf16[1,320,128]{2,1,0:T(8,128)(2,1)S(1)}, u32[]{:S(2)}, u32[]{:S(2)}) collective-permute-start(bf16[1,320,128]{2,1,0:T(8,128)(2,1)S(1)} %maximum_bitcast_fusion.1), channel_id=1, source_target_pairs={{0,4},{1,5},{2,6},{3,7},{4,0},{5,1},{6,2},{7,3},{8,12},{9,13},{10,... | collective-permute-start | bytes 245768 | tf_op jit(solution)/shard_map/ppermute | solution.py:61
  7.1 9.7 %collective-permute-start.10 = (bf16[1,320,128]{2,1,0:T(8,128)(2,1)S(1)}, bf16[1,320,128]{2,1,0:T(8,128)(2,1)S(1)}, u32[]{:S(2)}, u32[]{:S(2)}) collective-permute-start(bf16[1,320,128]{2,1,0:T(8,128)(2,1)S(1)} %maximum_bitcast_fusion.2), channel_id=1, source_target_pairs={{0,16},{8,24},{16,0},{24,8},{1,17},{9,25},{17,1},{25,9},{2,18},{10... | collective-permute-start | bytes 245768 | tf_op jit(solution)/shard_map/ppermute | solution.py:61
  15.1 9.2 %collective-permute-start.5 = (bf16[2,384,128]{2,1,0:T(8,128)(2,1)S(1)}, bf16[2,384,128]{2,1,0:T(8,128)(2,1)S(1)}, u32[]{:S(2)}, u32[]{:S(2)}) collective-permute-start(bf16[2,384,128]{2,1,0:T(8,128)(2,1)S(1)} %pad_maximum_fusion.10), channel_id=1, source_target_pairs={{0,2},{1,3},{2,0},{3,1},{4,6},{5,7},{6,4},{7,5},{8,10},{9,11},{10,... | collective-permute-start | bytes 589832 | tf_op jit(solution)/shard_map/ppermute | solution.py:61
  16.8 9.7 %collective-permute-start.11 = (bf16[2,320,128]{2,1,0:T(8,128)(2,1)S(1)}, bf16[2,320,128]{2,1,0:T(8,128)(2,1)S(1)}, u32[]{:S(2)}, u32[]{:S(2)}) collective-permute-start(bf16[2,320,128]{2,1,0:T(8,128)(2,1)S(1)} %pad_maximum_fusion.12), channel_id=1, source_target_pairs={{0,4},{1,5},{2,6},{3,7},{4,0},{5,1},{6,2},{7,3},{8,12},{9,13},{10,... | collective-permute-start | bytes 491528 | tf_op jit(solution)/shard_map/ppermute | solution.py:61
  24.3 11.5 %collective-permute-start.6 = (bf16[4,384,128]{2,1,0:T(8,128)(2,1)S(1)}, bf16[4,384,128]{2,1,0:T(8,128)(2,1)S(1)}, u32[]{:S(2)}, u32[]{:S(2)}) collective-permute-start(bf16[4,384,128]{2,1,0:T(8,128)(2,1)S(1)} %pad_maximum_fusion.6), channel_id=1, source_target_pairs={{0,1},{1,0},{2,3},{3,2},{4,5},{5,4},{6,7},{7,6},{8,9},{9,8},{10,11... | collective-permute-start | bytes 1179656 | tf_op jit(solution)/shard_map/ppermute | solution.py:61
  25.9 8.0 %collective-permute-start.1 = (bf16[2,320,128]{2,1,0:T(8,128)(2,1)S(1)}, bf16[2,320,128]{2,1,0:T(8,128)(2,1)S(1)}, u32[]{:S(2)}, u32[]{:S(2)}) collective-permute-start(bf16[2,320,128]{2,1,0:T(8,128)(2,1)S(1)} %pad_maximum_fusion.11), channel_id=1, source_target_pairs={{0,1},{1,0},{2,3},{3,2},{4,5},{5,4},{6,7},{7,6},{8,9},{9,8},{10,11... | collective-permute-start | bytes 491528 | tf_op jit(solution)/shard_map/ppermute | solution.py:61
  26.5 9.3 %copy-start.37 = (bf16[2,320,128]{2,1,0:T(8,128)(2,1)}, bf16[2,320,128]{2,1,0:T(8,128)(2,1)S(1)}, u32[]{:S(2)}) copy-start(bf16[2,320,128]{2,1,0:T(8,128)(2,1)S(1)} %collective-permute-done.11) | copy-start | bytes 491524
  27.3 20.2 %collective-permute-start.12 = (bf16[4,320,128]{2,1,0:T(8,128)(2,1)}, bf16[4,320,128]{2,1,0:T(8,128)(2,1)}, u32[]{:S(2)}, u32[]{:S(2)}) collective-permute-start(bf16[4,320,128]{2,1,0:T(8,128)(2,1)} %pad_maximum_fusion.8), channel_id=1, source_target_pairs={{0,2},{1,3},{2,0},{3,1},{4,6},{5,7},{6,4},{7,5},{8,10},{9,11},{10,... | collective-permute-start | bytes 983048 | tf_op jit(solution)/shard_map/ppermute | solution.py:61
  34.7 4.4 %copy-start.51 = (s32[8,64,2]{1,2,0:T(2,128)S(1)}, s32[8,64,2]{1,2,0:T(2,128)}, u32[]{:S(2)}) copy-start(s32[8,64,2]{1,2,0:T(2,128)} %param.31) | copy-start | bytes 12292
  34.7 4.8 %copy-start.53 = (s32[8,64]{1,0:T(8,128)S(1)}, s32[8,64]{1,0:T(8,128)}, u32[]{:S(2)}) copy-start(s32[8,64]{1,0:T(8,128)} %param.33) | copy-start | bytes 6148
  34.7 5.0 %copy-start.50 = (f32[8,64,2]{1,2,0:T(2,128)S(1)}, f32[8,64,2]{1,2,0:T(2,128)}, u32[]{:S(2)}) copy-start(f32[8,64,2]{1,2,0:T(2,128)} %param.32) | copy-start | bytes 12292
  34.7 15.5 %collective-permute-start.2 = (bf16[4,320,128]{2,1,0:T(8,128)(2,1)}, bf16[4,320,128]{2,1,0:T(8,128)(2,1)}, u32[]{:S(2)}, u32[]{:S(2)}) collective-permute-start(bf16[4,320,128]{2,1,0:T(8,128)(2,1)} %pad_maximum_fusion.7), channel_id=1, source_target_pairs={{0,16},{8,24},{16,0},{24,8},{1,17},{9,25},{17,1},{25,9},{2,18},{10... | collective-permute-start | bytes 983048 | tf_op jit(solution)/shard_map/ppermute | solution.py:61
  35.9 18.7 %copy-start.12 = (bf16[8,384,128]{2,1,0:T(8,128)(2,1)}, bf16[8,384,128]{2,1,0:T(8,128)(2,1)S(1)}, u32[]{:S(2)}) copy-start(bf16[8,384,128]{2,1,0:T(8,128)(2,1)S(1)} %pad_maximum_fusion.2.refs_4_) | copy-start | bytes 2359300
  35.9 19.4 %collective-permute-start.7 = (bf16[8,384,128]{2,1,0:T(8,128)(2,1)S(1)}, bf16[8,384,128]{2,1,0:T(8,128)(2,1)}, u32[]{:S(2)}, u32[]{:S(2)}) collective-permute-start(bf16[8,384,128]{2,1,0:T(8,128)(2,1)S(1)} %pad_maximum_fusion.2.refs_4_), channel_id=1, source_target_pairs={{0,16},{8,24},{16,0},{24,8},{1,17},{9,25},{17,1},{25,9},{2,18},{10... | collective-permute-start | bytes 2359304 | tf_op jit(solution)/shard_map/ppermute | solution.py:61
  47.5 5.3 %copy-start.44 = (f32[64,512]{1,0:T(8,128)S(1)}, f32[64,512]{1,0:T(8,128)}, u32[]{:S(2)}) copy-start(f32[64,512]{1,0:T(8,128)} %fusion.20) | copy-start | bytes 393220
  48.6 6.0 %copy-start.15 = (bf16[8,320,128]{2,1,0:T(8,128)(2,1)}, bf16[8,320,128]{2,1,0:T(8,128)(2,1)S(1)}, u32[]{:S(2)}) copy-start(bf16[8,320,128]{2,1,0:T(8,128)(2,1)S(1)} %pad_maximum_fusion.4.refs_8_) | copy-start | bytes 1966084
  48.6 21.1 %collective-permute-start.13 = (bf16[8,320,128]{2,1,0:T(8,128)(2,1)S(1)}, bf16[8,320,128]{2,1,0:T(8,128)(2,1)S(1)}, u32[]{:S(2)}, u32[]{:S(2)}) collective-permute-start(bf16[8,320,128]{2,1,0:T(8,128)(2,1)S(1)} %pad_maximum_fusion.4.refs_8_), channel_id=1, source_target_pairs={{0,1},{1,0},{2,3},{3,2},{4,5},{5,4},{6,7},{7,6},{8,9},{9,8},{10,11... | collective-permute-start | bytes 1966088 | tf_op jit(solution)/shard_map/ppermute | solution.py:61
  50.2 20.0 %collective-permute-start.14 = (bf16[8,320,128]{2,1,0:T(8,128)(2,1)S(1)}, bf16[8,320,128]{2,1,0:T(8,128)(2,1)S(1)}, u32[]{:S(2)}, u32[]{:S(2)}) collective-permute-start(bf16[8,320,128]{2,1,0:T(8,128)(2,1)S(1)} %pad_maximum_fusion.4.refs_8_), channel_id=1, source_target_pairs={{0,8},{8,0},{16,24},{24,16},{1,9},{9,1},{17,25},{25,17},{2,10},{10... | collective-permute-start | bytes 1966088 | tf_op jit(solution)/shard_map/ppermute | solution.py:61
  51.2 17.2 %copy-start.16 = (bf16[8,320,128]{2,1,0:T(8,128)(2,1)}, bf16[8,320,128]{2,1,0:T(8,128)(2,1)S(1)}, u32[]{:S(2)}) copy-start(bf16[8,320,128]{2,1,0:T(8,128)(2,1)S(1)} %pad_maximum_fusion.3.refs_12_) | copy-start | bytes 1966084
  51.2 17.2 %collective-permute-start.3 = (bf16[8,320,128]{2,1,0:T(8,128)(2,1)S(1)}, bf16[8,320,128]{2,1,0:T(8,128)(2,1)S(1)}, u32[]{:S(2)}, u32[]{:S(2)}) collective-permute-start(bf16[8,320,128]{2,1,0:T(8,128)(2,1)S(1)} %pad_maximum_fusion.3.refs_12_), channel_id=1, source_target_pairs={{0,2},{1,3},{2,0},{3,1},{4,6},{5,7},{6,4},{7,5},{8,10},{9,11},{10,... | collective-permute-start | bytes 1966088 | tf_op jit(solution)/shard_map/ppermute | solution.py:61
  54.6 16.0 %collective-permute-start.8 = (bf16[8,384,128]{2,1,0:T(8,128)(2,1)S(1)}, bf16[8,384,128]{2,1,0:T(8,128)(2,1)S(1)}, u32[]{:S(2)}, u32[]{:S(2)}) collective-permute-start(bf16[8,384,128]{2,1,0:T(8,128)(2,1)S(1)} %pad_maximum_fusion.2.refs_4_), channel_id=1, source_target_pairs={{0,8},{8,0},{16,24},{24,16},{1,9},{9,1},{17,25},{25,17},{2,10},{10... | collective-permute-start | bytes 2359304 | tf_op jit(solution)/shard_map/ppermute | solution.py:61
  55.3 18.4 %collective-permute-start.9 = (bf16[8,384,128]{2,1,0:T(8,128)(2,1)}, bf16[8,384,128]{2,1,0:T(8,128)(2,1)}, u32[]{:S(2)}, u32[]{:S(2)}) collective-permute-start(bf16[8,384,128]{2,1,0:T(8,128)(2,1)} %collective-permute-done.7.refs_5_), channel_id=1, source_target_pairs={{0,8},{8,0},{16,24},{24,16},{1,9},{9,1},{17,25},{25,17},{2,10},{10... | collective-permute-start | bytes 2359304 | tf_op jit(solution)/shard_map/ppermute | solution.py:61
  68.4 4.4 %copy-start.33 = (bf16[8,320,128]{2,1,0:T(8,128)(2,1)}, bf16[8,320,128]{2,1,0:T(8,128)(2,1)S(1)}, u32[]{:S(2)}) copy-start(bf16[8,320,128]{2,1,0:T(8,128)(2,1)S(1)} %collective-permute-done.3.refs_13_) | copy-start | bytes 1966084
  68.4 2.1 collective-permute-start.16
  69.7 2.2 collective-permute-start.17
  70.2 2.7 collective-permute-start.15
  156.4 3.7 collective-permute-start.23
  156.9 7.2 %collective-permute-start.18 = (bf16[16,368,128]{2,1,0:T(8,128)(2,1)}, bf16[16,368,128]{2,1,0:T(8,128)(2,1)S(1)}, u32[]{:S(2)}, u32[]{:S(2)}) collective-permute-start(bf16[16,368,128]{2,1,0:T(8,128)(2,1)} %get-tuple-element.59), channel_id=1, source_target_pairs={{0,8},{8,0},{16,24},{24,16},{1,9},{9,1},{17,25},{25,17},{2,10},{10... | collective-permute-start | bytes 4521992 | tf_op jit(solution)/shard_map/ppermute | solution.py:61
  157.0 8.1 %collective-permute-start.28 = (bf16[16,384,128]{2,1,0:T(8,128)(2,1)}, bf16[16,384,128]{2,1,0:T(8,128)(2,1)S(1)}, u32[]{:S(2)}, u32[]{:S(2)}) collective-permute-start(bf16[16,384,128]{2,1,0:T(8,128)(2,1)} %get-tuple-element.64), channel_id=1, source_target_pairs={{0,8},{8,0},{16,24},{24,16},{1,9},{9,1},{17,25},{25,17},{2,10},{10... | collective-permute-start | bytes 4718600 | tf_op jit(solution)/shard_map/ppermute | solution.py:61
  162.5 19.2 %collective-permute-start.24 = (bf16[8,368,128]{2,1,0:T(8,128)(2,1)S(1)}, bf16[8,368,128]{2,1,0:T(8,128)(2,1)S(1)}, u32[]{:S(2)}, u32[]{:S(2)}) collective-permute-start(bf16[8,368,128]{2,1,0:T(8,128)(2,1)S(1)} %slice.535), channel_id=1, source_target_pairs={{0,2},{1,3},{2,0},{3,1},{4,6},{5,7},{6,4},{7,5},{8,10},{9,11},{10,... | collective-permute-start | bytes 2261000 | tf_op jit(solution)/shard_map/ppermute | solution.py:61
  164.5 18.9 %collective-permute-start.19 = (bf16[8,368,128]{2,1,0:T(8,128)(2,1)S(1)}, bf16[8,368,128]{2,1,0:T(8,128)(2,1)S(1)}, u32[]{:S(2)}, u32[]{:S(2)}) collective-permute-start(bf16[8,368,128]{2,1,0:T(8,128)(2,1)S(1)} %slice.536), channel_id=1, source_target_pairs={{0,1},{1,0},{2,3},{3,2},{4,5},{5,4},{6,7},{7,6},{8,9},{9,8},{10,11... | collective-permute-start | bytes 2261000 | tf_op jit(solution)/shard_map/ppermute | solution.py:61
  166.4 20.5 %collective-permute-start.29 = (bf16[8,384,128]{2,1,0:T(8,128)(2,1)S(1)}, bf16[8,384,128]{2,1,0:T(8,128)(2,1)S(1)}, u32[]{:S(2)}, u32[]{:S(2)}) collective-permute-start(bf16[8,384,128]{2,1,0:T(8,128)(2,1)S(1)} %slice.534), channel_id=1, source_target_pairs={{0,16},{8,24},{16,0},{24,8},{1,17},{9,25},{17,1},{25,9},{2,18},{10... | collective-permute-start | bytes 2359304 | tf_op jit(solution)/shard_map/ppermute | solution.py:61
  181.9 12.2 %collective-permute-start.25 = (bf16[4,368,128]{2,1,0:T(8,128)(2,1)S(1)}, bf16[4,368,128]{2,1,0:T(8,128)(2,1)S(1)}, u32[]{:S(2)}, u32[]{:S(2)}) collective-permute-start(bf16[4,368,128]{2,1,0:T(8,128)(2,1)S(1)} %slice.538), channel_id=1, source_target_pairs={{0,16},{8,24},{16,0},{24,8},{1,17},{9,25},{17,1},{25,9},{2,18},{10... | collective-permute-start | bytes 1130504 | tf_op jit(solution)/shard_map/ppermute | solution.py:61
  183.5 11.3 %collective-permute-start.20 = (bf16[4,368,128]{2,1,0:T(8,128)(2,1)S(1)}, bf16[4,368,128]{2,1,0:T(8,128)(2,1)S(1)}, u32[]{:S(2)}, u32[]{:S(2)}) collective-permute-start(bf16[4,368,128]{2,1,0:T(8,128)(2,1)S(1)} %slice.539), channel_id=1, source_target_pairs={{0,2},{1,3},{2,0},{3,1},{4,6},{5,7},{6,4},{7,5},{8,10},{9,11},{10,... | collective-permute-start | bytes 1130504 | tf_op jit(solution)/shard_map/ppermute | solution.py:61
  187.2 13.7 %collective-permute-start.30 = (bf16[4,384,128]{2,1,0:T(8,128)(2,1)S(1)}, bf16[4,384,128]{2,1,0:T(8,128)(2,1)S(1)}, u32[]{:S(2)}, u32[]{:S(2)}) collective-permute-start(bf16[4,384,128]{2,1,0:T(8,128)(2,1)S(1)} %slice.537), channel_id=1, source_target_pairs={{0,1},{1,0},{2,3},{3,2},{4,5},{5,4},{6,7},{7,6},{8,9},{9,8},{10,11... | collective-permute-start | bytes 1179656 | tf_op jit(solution)/shard_map/ppermute | solution.py:61
  194.2 10.4 %collective-permute-start.26 = (f32[2,368,128]{2,1,0:T(8,128)S(1)}, f32[2,368,128]{2,1,0:T(8,128)S(1)}, u32[]{:S(2)}, u32[]{:S(2)}) collective-permute-start(f32[2,368,128]{2,1,0:T(8,128)S(1)} %slice.416), channel_id=1, source_target_pairs={{0,1},{1,0},{2,3},{3,2},{4,5},{5,4},{6,7},{7,6},{8,9},{9,8},{10,11... | collective-permute-start | bytes 1130504 | tf_op jit(solution)/shard_map/ppermute | solution.py:61
  194.9 23.4 %collective-permute-start.21 = (f32[2,368,128]{2,1,0:T(8,128)S(1)}, f32[2,368,128]{2,1,0:T(8,128)S(1)}, u32[]{:S(2)}, u32[]{:S(2)}) collective-permute-start(f32[2,368,128]{2,1,0:T(8,128)S(1)} %slice.407), channel_id=1, source_target_pairs={{0,4},{1,5},{2,6},{3,7},{4,0},{5,1},{6,2},{7,3},{8,12},{9,13},{10,... | collective-permute-start | bytes 1130504 | tf_op jit(solution)/shard_map/ppermute | solution.py:61
  200.9 18.6 %collective-permute-start.31 = (f32[2,384,128]{2,1,0:T(8,128)S(1)}, f32[2,384,128]{2,1,0:T(8,128)S(1)}, u32[]{:S(2)}, u32[]{:S(2)}) collective-permute-start(f32[2,384,128]{2,1,0:T(8,128)S(1)} %slice.425), channel_id=1, source_target_pairs={{0,2},{1,3},{2,0},{3,1},{4,6},{5,7},{6,4},{7,5},{8,10},{9,11},{10,... | collective-permute-start | bytes 1179656 | tf_op jit(solution)/shard_map/ppermute | solution.py:61
  204.7 24.7 %collective-permute-start.27 = (f32[1,368,128]{2,1,0:T(8,128)S(1)}, f32[1,368,128]{2,1,0:T(8,128)S(1)}, u32[]{:S(2)}, u32[]{:S(2)}) collective-permute-start(f32[1,368,128]{2,1,0:T(8,128)S(1)} %slice.418), channel_id=1, source_target_pairs={{0,4},{1,5},{2,6},{3,7},{4,0},{5,1},{6,2},{7,3},{8,12},{9,13},{10,... | collective-permute-start | bytes 565256 | tf_op jit(solution)/shard_map/ppermute | solution.py:61
  218.4 11.7 %collective-permute-start.22 = (f32[1,368,128]{2,1,0:T(8,128)S(1)}, f32[1,368,128]{2,1,0:T(8,128)S(1)}, u32[]{:S(2)}, u32[]{:S(2)}) collective-permute-start(f32[1,368,128]{2,1,0:T(8,128)S(1)} %slice.409), channel_id=1, source_target_pairs={{0,16},{8,24},{16,0},{24,8},{1,17},{9,25},{17,1},{25,9},{2,18},{10... | collective-permute-start | bytes 565256 | tf_op jit(solution)/shard_map/ppermute | solution.py:61
  219.7 13.6 %collective-permute-start.32 = (f32[1,384,128]{2,1,0:T(8,128)S(1)}, f32[1,384,128]{2,1,0:T(8,128)S(1)}, u32[]{:S(2)}, u32[]{:S(2)}) collective-permute-start(f32[1,384,128]{2,1,0:T(8,128)S(1)} %slice.427), channel_id=1, source_target_pairs={{0,4},{1,5},{2,6},{3,7},{4,0},{5,1},{6,2},{7,3},{8,12},{9,13},{10,... | collective-permute-start | bytes 589832 | tf_op jit(solution)/shard_map/ppermute | solution.py:61
  235.9 4.2 %collective-permute-start.33 = (f32[1,104,128]{2,1,0:T(8,128)S(1)}, f32[1,104,128]{2,1,0:T(8,128)S(1)}, u32[]{:S(2)}, u32[]{:S(2)}) collective-permute-start(f32[1,104,128]{2,1,0:T(8,128)S(1)} %fusion.26), channel_id=1, source_target_pairs={{0,16},{8,24},{16,0},{24,8},{1,17},{9,25},{17,1},{25,9},{2,18},{10... | collective-permute-start | bytes 159752 | tf_op jit(solution)/shard_map/ppermute | solution.py:61
  240.1 4.8 %collective-permute-start.34 = (f32[2,104,128]{2,1,0:T(8,128)S(1)}, f32[2,104,128]{2,1,0:T(8,128)S(1)}, u32[]{:S(2)}, u32[]{:S(2)}) collective-permute-start(f32[2,104,128]{2,1,0:T(8,128)S(1)} %pad_maximum_fusion.13), channel_id=1, source_target_pairs={{0,2},{1,3},{2,0},{3,1},{4,6},{5,7},{6,4},{7,5},{8,10},{9,11},{10,... | collective-permute-start | bytes 319496 | tf_op jit(solution)/shard_map/ppermute | solution.py:61
  244.9 5.9 %collective-permute-start.35 = (f32[4,104,128]{2,1,0:T(8,128)S(1)}, f32[4,104,128]{2,1,0:T(8,128)S(1)}, u32[]{:S(2)}, u32[]{:S(2)}) collective-permute-start(f32[4,104,128]{2,1,0:T(8,128)S(1)} %pad_maximum_fusion.9), channel_id=1, source_target_pairs={{0,1},{1,0},{2,3},{3,2},{4,5},{5,4},{6,7},{7,6},{8,9},{9,8},{10,11... | collective-permute-start | bytes 638984 | tf_op jit(solution)/shard_map/ppermute | solution.py:61
  247.2 11.8 %collective-permute-start.38 = (f32[1,1024,128]{2,1,0:T(8,128)}, f32[1,1024,128]{2,1,0:T(8,128)}, u32[]{:S(2)}, u32[]{:S(2)}) collective-permute-start(f32[1,1024,128]{2,1,0:T(8,128)} %bitcast.38), channel_id=1, source_target_pairs={{0,16},{8,24},{16,0},{24,8},{1,17},{9,25},{17,1},{25,9},{2,18},{10... | collective-permute-start | bytes 1572872 | tf_op jit(solution)/shard_map/ppermute | solution.py:61
  250.8 18.5 %collective-permute-start.36 = (f32[8,104,128]{2,1,0:T(8,128)S(1)}, f32[8,104,128]{2,1,0:T(8,128)S(1)}, u32[]{:S(2)}, u32[]{:S(2)}) collective-permute-start(f32[8,104,128]{2,1,0:T(8,128)S(1)} %pad_maximum_fusion.5), channel_id=1, source_target_pairs={{0,4},{1,5},{2,6},{3,7},{4,0},{5,1},{6,2},{7,3},{8,12},{9,13},{10,... | collective-permute-start | bytes 1277960 | tf_op jit(solution)/shard_map/ppermute | solution.py:61
  253.7 16.7 %copy-start.1 = (f32[24,128,128]{2,1,0:T(8,128)S(1)}, f32[24,128,128]{2,1,0:T(8,128)}, u32[]{:S(2)}) copy-start(f32[24,128,128]{2,1,0:T(8,128)} %param.41) | copy-start | bytes 4718596
  253.7 16.7 %copy-start.3 = (f32[24,128,128]{2,1,0:T(8,128)S(1)}, f32[24,128,128]{2,1,0:T(8,128)}, u32[]{:S(2)}) copy-start(f32[24,128,128]{2,1,0:T(8,128)} %param.40) | copy-start | bytes 4718596
  261.2 10.5 %collective-permute-start.39 = (f32[2,1024,128]{2,1,0:T(8,128)}, f32[2,1024,128]{2,1,0:T(8,128)}, u32[]{:S(2)}, u32[]{:S(2)}) collective-permute-start(f32[2,1024,128]{2,1,0:T(8,128)} %pad_maximum_fusion.1), channel_id=1, source_target_pairs={{0,8},{8,0},{16,24},{24,16},{1,9},{9,1},{17,25},{25,17},{2,10},{10... | collective-permute-start | bytes 3145736 | tf_op jit(solution)/shard_map/ppermute | solution.py:61
  270.3 8.0 %collective-permute-start.37 = (f32[16,104,128]{2,1,0:T(8,128)}, f32[16,104,128]{2,1,0:T(8,128)}, u32[]{:S(2)}, u32[]{:S(2)}) collective-permute-start(f32[16,104,128]{2,1,0:T(8,128)} %get-tuple-element.94), channel_id=1, source_target_pairs={{0,8},{8,0},{16,24},{24,16},{1,9},{9,1},{17,25},{25,17},{2,10},{10... | collective-permute-start | bytes 2555912 | tf_op jit(solution)/shard_map/ppermute | solution.py:61
  290.6 9.6 %copy-start.19 = (f32[4,256,128]{2,1,0:T(8,128)S(1)}, f32[4,256,128]{2,1,0:T(8,128)}, u32[]{:S(2)}) copy-start(f32[4,256,128]{2,1,0:T(8,128)} %slice_multiply_fusion.2) | copy-start | bytes 1572868
  290.7 10.8 %copy-start.4 = (f32[24,128,128]{2,1,0:T(8,128)S(1)}, f32[24,128,128]{2,1,0:T(8,128)}, u32[]{:S(2)}) copy-start(f32[24,128,128]{2,1,0:T(8,128)} %param.40) | copy-start | bytes 4718596
  308.1 5.3 %copy-start.6 = (f32[24,128,128]{2,1,0:T(8,128)}, f32[24,128,128]{2,1,0:T(8,128)S(1)}, u32[]{:S(2)}) copy-start(f32[24,128,128]{2,1,0:T(8,128)S(1)} %multiply_add_fusion) | copy-start | bytes 4718596
  313.4 30.3 %copy-start.2 = (f32[512,640]{1,0:T(8,128)S(1)}, f32[512,640]{1,0:T(8,128)}, u32[]{:S(2)}) copy-start(f32[512,640]{1,0:T(8,128)} %slice_dynamic-update-slice_fusion) | copy-start | bytes 3932164
  341.9 21.4 %collective-permute-start.40 = (f32[24,128,128]{2,1,0:T(8,128)}, f32[24,128,128]{2,1,0:T(8,128)}, u32[]{:S(2)}, u32[]{:S(2)}) collective-permute-start(f32[24,128,128]{2,1,0:T(8,128)} %renew.1), channel_id=1, source_target_pairs={{0,8},{8,0},{16,24},{24,16},{1,9},{9,1},{17,25},{25,17},{2,10},{10... | collective-permute-start | bytes 4718600 | tf_op jit(solution)/shard_map/ppermute | solution.py:61
  345.0 4.7 %copy-start.41 = (f32[513,255]{1,0:T(8,128)S(1)}, f32[513,255]{1,0:T(8,128)}, u32[]{:S(2)}) copy-start(f32[513,255]{1,0:T(8,128)} %param.51) | copy-start | bytes 1569784
  345.0 6.4 %copy-start.30 = (f32[256,512]{1,0:T(8,128)S(1)}, f32[256,512]{1,0:T(8,128)}, u32[]{:S(2)}) copy-start(f32[256,512]{1,0:T(8,128)} %param.42) | copy-start | bytes 1572868
  345.0 6.4 %copy-start.42 = (f32[256,512]{1,0:T(8,128)S(1)}, f32[256,512]{1,0:T(8,128)}, u32[]{:S(2)}) copy-start(f32[256,512]{1,0:T(8,128)} %param.43) | copy-start | bytes 1572868
  345.0 6.4 %copy-start.43 = (f32[256,512]{1,0:T(8,128)S(1)}, f32[256,512]{1,0:T(8,128)}, u32[]{:S(2)}) copy-start(f32[256,512]{1,0:T(8,128)} %param.44) | copy-start | bytes 1572868
  358.7 4.5 %copy-start.8 = (f32[24,128,128]{2,1,0:T(8,128)S(1)}, f32[24,128,128]{2,1,0:T(8,128)}, u32[]{:S(2)}) copy-start(f32[24,128,128]{2,1,0:T(8,128)} %renew.1) | copy-start | bytes 4718596
  (34 other events, 82.3 us)

commit v2 on v1

--- a/solution.py
+++ b/solution.py
@@ -126,7 +126,7 @@
     return jnp.stack(units), jnp.stack(spots)
 
 
-def gathered_pieces(blocks_low, maps_low, ready, dp, fsdp):
+def gathered_pieces(blocks_low, maps_low, dp, fsdp):
     dp_here = lax.axis_index("dp")
     quarter = blocks_low.shape[0] // dp
     piece_rows = maps_low.shape[0] // dp
@@ -140,13 +140,9 @@
             0,
         )
         held = gather_doubling(piece, order[2:])
-        pieces.append([held, swap(held, *order[1])])
-    pieces[-1][1], ready = lax.optimization_barrier((pieces[-1][1], ready))
-    return [
-        piece
-        for both, order in zip(pieces, part_orders(dp, fsdp))
-        for piece in both + [swap(piece, *order[0]) for piece in both]
-    ], ready
+        both = [held, swap(held, *order[1])]
+        pieces += both + [swap(piece, *order[0]) for piece in both]
+    return pieces
 
 
 def reduced_grads(outs, sums, slots, map_rows, dp, fsdp):
@@ -165,7 +161,7 @@
     dp_here = lax.axis_index("dp")
     fsdp_here = lax.axis_index("fsdp")
     parts = [
-        scatter_sum(outs[2 * part], outs[2 * part + 1], order, 2)
+        scatter_sum(outs[2 * part], outs[2 * part + 1], order, 1)
         for part, order in enumerate(part_orders(dp, fsdp))
     ]
     cut = 2 * BS
@@ -745,7 +741,7 @@
         head_wide, jnp.broadcast_to(head_bias, (8, HEAD_COLS)),
     )
     if fast:
-        sources, inputs = gathered_pieces(blocks_low, maps_low, inputs, dp, fsdp)
+        sources = gathered_pieces(blocks_low, maps_low, dp, fsdp)
     *outs, sums = pl.pallas_call(
         functools.partial(model_kernel, fast, PART_ROWS),
         out_shape=[jax.ShapeDtypeStruct(shape, kind) for shape, kind in shapes],

time: 373 us -> 360 us (0.965)
  waiting for transfers between devices: 93.1 us -> 81 us
    ppermute x41, waiting for transfers between devices: 93.1 us -> 81 us  [swap(): return lax.ppermute(value, axis, [(i, i ^ bit) for i in range(size)])]
    unnamed x132 -> x114, local copies, waits for them, and re-layouts: 19.3 us -> 17.7 us
  transfers between devices with their start and end apart: 41 -> 41, of which waited for: 21 -> 19; matrix products, arithmetic and copies ran while one was open for 18% -> 17% of each run, Pallas kernels for 0% -> 0%
where the time goes in v2:
time: 360 us; the launch traced here: 353 us
  Pallas kernels  111 us (31%)
  waiting for transfers between devices  81 us (22%)
  local copies, waits for them, and re-layouts  46.2 us (13%)
  starting transfers between devices  45.5 us (13%)
  other arithmetic  35.9 us (10%)
  matrix products  22.9 us (6%)
  between operations  10.5 us (3%)
    pallas_call x1, Pallas kernels, model_grads(): pl.pallas_call(functools.partial(model_kernel, fast, PART_ROWS), out_shap...  82.9 us
    ppermute x41, waiting for transfers between devices, swap(): return lax.ppermute(value, axis, [(i, i ^ bit) for i in range(size)])  81 us
    ppermute x41, starting transfers between devices, swap(): return lax.ppermute(value, axis, [(i, i ^ bit) for i in range(size)])  45.5 us
    pallas_call x1, Pallas kernels, renew_all(): pl.pallas_call(functools.partial(qr_kernel, count), out_shape=jax.ShapeDt...  28.5 us
    unnamed x114, local copies, waits for them, and re-layouts  17.7 us
  transfers between devices with their start and end apart: 41, of which 19 were waited for; matrix products, arithmetic and copies ran while one was open for 17% of the time, Pallas kernels for 0%

profile of v2, /device:TPU:0, one launch (start us, length us, event | category | flops | bytes accessed | tf_op | source)
XLA Modules:
  0.0 353.5 jit_solution(12960804252221556173)
XLA Ops:
  2.9 4.1 %collective-permute-start.12 = (bf16[1,320,128]{2,1,0:T(8,128)(2,1)S(1)}, bf16[1,320,128]{2,1,0:T(8,128)(2,1)S(1)}, u32[]{:S(2)}, u32[]{:S(2)}) collective-permute-start(bf16[1,320,128]{2,1,0:T(8,128)(2,1)S(1)} %maximum_bitcast_fusion.2), channel_id=1, source_target_pairs={{0,4},{1,5},{2,6},{3,7},{4,0},{5,1},{6,2},{7,3},{8,12},{9,13},{10,... | collective-permute-start | bytes 245768 | tf_op jit(solution)/shard_map/ppermute | solution.py:61
  7.0 1.5 collective-permute-start.6
  10.1 1.6 gather_fusion
  14.2 1.4 slice_select_fusion.refs_24_
  15.7 1.6 collective-permute-start.1
  17.3 1.6 collective-permute-start.13
  18.9 2.7 collective-permute-start.7
  22.7 3.1 collective-permute-start.2
  25.9 2.9 collective-permute-start.14
  29.0 2.6 collective-permute-done.2
  31.6 2.9 collective-permute-start.3
  34.5 2.9 collective-permute-done.14
  37.7 1.9 collective-permute-done.8
  41.8 8.9 %collective-permute-done.3.refs_5_ = bf16[8,384,128]{2,1,0:T(8,128)(2,1)} collective-permute-done((bf16[8,384,128]{2,1,0:T(8,128)(2,1)S(1)}, bf16[8,384,128]{2,1,0:T(8,128)(2,1)}, u32[]{:S(2)}, u32[]{:S(2)}) %collective-permute-start.3) | collective-permute-done | bytes 786464 | tf_op jit(solution)/shard_map/ppermute | solution.py:61
  51.4 3.7 %collective-permute-done.9.refs_9_ = bf16[8,320,128]{2,1,0:T(8,128)(2,1)} collective-permute-done((bf16[8,320,128]{2,1,0:T(8,128)(2,1)S(1)}, bf16[8,320,128]{2,1,0:T(8,128)(2,1)}, u32[]{:S(2)}, u32[]{:S(2)}) %collective-permute-start.9) | collective-permute-done | bytes 655392 | tf_op jit(solution)/shard_map/ppermute | solution.py:61
  58.9 1.7 fusion.1
  60.7 2.0 concatenate.139.refs_25_
  64.9 1.6 convolution_add_fusion.refs_19_
  67.7 82.9 %model.1 = (f32[16,384,128]{2,1,0:T(8,128)}, bf16[16,384,128]{2,1,0:T(8,128)(2,1)}, f32[16,368,128]{2,1,0:T(8,128)}, bf16[16,368,128]{2,1,0:T(8,128)(2,1)}, f32[...) custom-call(s32[192]{0:T(256)} %refs_0_.1, s32[96]{0:T(128)} %reshape.1024.refs_1_, ...), custom_call_target="tpu_custom_call" | custom-call | tf_op jit(solution)/shard_map/model/pallas_call | solution.py:745
  151.7 2.6 collective-permute-done.23
  154.4 2.3 convert_add_fusion.1
  156.8 2.0 collective-permute-start.24
  161.1 2.1 collective-permute-start.29
  164.0 12.1 %collective-permute-done.24 = bf16[8,368,128]{2,1,0:T(8,128)(2,1)S(1)} collective-permute-done((bf16[8,368,128]{2,1,0:T(8,128)(2,1)S(1)}, bf16[8,368,128]{2,1,0:T(8,128)(2,1)S(1)}, u32[]{:S(2)}, u32[]{:S(2)}) %collective-permute-start.24) | collective-permute-done | bytes 753696 | tf_op jit(solution)/shard_map/ppermute | solution.py:61
  176.3 2.1 collective-permute-start.25
  178.7 1.8 collective-permute-start.20
  182.5 6.6 %collective-permute-done.25 = bf16[4,368,128]{2,1,0:T(8,128)(2,1)S(1)} collective-permute-done((bf16[4,368,128]{2,1,0:T(8,128)(2,1)S(1)}, bf16[4,368,128]{2,1,0:T(8,128)(2,1)S(1)}, u32[]{:S(2)}, u32[]{:S(2)}) %collective-permute-start.25) | collective-permute-done | bytes 376864 | tf_op jit(solution)/shard_map/ppermute | solution.py:61
  189.7 2.4 collective-permute-start.21
  192.5 1.3 collective-permute-start.31
  193.8 2.1 collective-permute-done.26
  197.0 5.6 %collective-permute-done.21 = bf16[2,368,128]{2,1,0:T(8,128)(2,1)S(1)} collective-permute-done((bf16[2,368,128]{2,1,0:T(8,128)(2,1)S(1)}, bf16[2,368,128]{2,1,0:T(8,128)(2,1)S(1)}, u32[]{:S(2)}, u32[]{:S(2)}) %collective-permute-start.21) | collective-permute-done | bytes 188448 | tf_op jit(solution)/shard_map/ppermute | solution.py:61
  202.7 1.4 collective-permute-start.22
  204.3 9.1 %collective-permute-done.27 = f32[1,368,128]{2,1,0:T(8,128)S(1)} collective-permute-done((f32[1,368,128]{2,1,0:T(8,128)S(1)}, f32[1,368,128]{2,1,0:T(8,128)S(1)}, u32[]{:S(2)}, u32[]{:S(2)}) %collective-permute-start.27) | collective-permute-done | bytes 188448 | tf_op jit(solution)/shard_map/ppermute | solution.py:61
  214.6 2.4 collective-permute-done.32
  219.8 1.5 collective-permute-start.33
  224.8 3.9 %collective-permute-done.34 = f32[2,104,128]{2,1,0:T(8,128)S(1)} collective-permute-done((f32[2,104,128]{2,1,0:T(8,128)S(1)}, f32[2,104,128]{2,1,0:T(8,128)S(1)}, u32[]{:S(2)}, u32[]{:S(2)}) %collective-permute-start.34) | collective-permute-done | bytes 106528 | tf_op jit(solution)/shard_map/ppermute | solution.py:61
  228.7 1.8 collective-permute-start.35
  231.2 1.4 collective-permute-start.38
  233.3 1.3 collective-permute-done.35
  234.7 1.6 collective-permute-start.36
  237.6 5.7 %collective-permute-done.38 = f32[1,1024,128]{2,1,0:T(8,128)} collective-permute-done((f32[1,1024,128]{2,1,0:T(8,128)}, f32[1,1024,128]{2,1,0:T(8,128)}, u32[]{:S(2)}, u32[]{:S(2)}) %collective-permute-start.38) | collective-permute-done | bytes 524320 | tf_op jit(solution)/shard_map/ppermute | solution.py:61
  243.3 2.2 pad_maximum_fusion.1
  246.3 7.0 %collective-permute-done.36 = f32[8,104,128]{2,1,0:T(8,128)S(1)} collective-permute-done((f32[8,104,128]{2,1,0:T(8,128)S(1)}, f32[8,104,128]{2,1,0:T(8,128)S(1)}, u32[]{:S(2)}, u32[]{:S(2)}) %collective-permute-start.36) | collective-permute-done | bytes 426016 | tf_op jit(solution)/shard_map/ppermute | solution.py:61
  254.4 1.3 broadcast_select_fusion.2.basis_ref
  255.7 3.0 pad_maximum_fusion
  258.7 3.6 %gather_fusion.2 = f32[4,1024,128]{2,1,0:T(8,128)} fusion(f32[4,1024,128]{2,1,0:T(8,128)} %pad_maximum_fusion, s32[1024]{0:T(1024)S(1)} %pad_clamp_fusion), kind=kCustom, calls=%fused_computation.2 | custom fusion | bytes 4194320 | tf_op jit(solution)/shard_map/gather | solution.py:178
  262.3 2.1 constant_dynamic-update-slice_fusion.5
  264.4 2.1 gather_fusion.1
  270.6 1.9 slice_multiply_fusion.2
  272.5 1.5 slice_multiply_fusion
  274.7 1.8 slice_dynamic-update-slice_fusion.3
  276.5 1.7 slice_dynamic-update-slice_fusion.2
  278.2 1.7 slice_dynamic-update-slice_fusion.1
  279.9 1.7 slice_dynamic-update-slice_fusion
  285.4 3.9 %fusion.72 = f32[24,128,128]{1,2,0:T(8,128)} fusion(f32[24,128,128]{2,1,0:T(8,128)S(1)} %bitcast.116, f32[24,128,128]{2,1,0:T(8,128)S(1)} %copy-done.4), kind=kOutput, calls=%fused_computation.276 | convolution fusion | flops 603979776 | bytes 4718592 | tf_op jit(solution)/shard_map/bji,bjk->bik/dot_general | solution.py:888
  289.4 2.7 multiply_add_fusion
  292.1 5.3 %broadcast_select_fusion.3 = (f32[24,128,128]{2,1,0:T(8,128)}, f32[24,128,128]{2,1,0:T(8,128)}) fusion(f32[24,128,128]{2,1,0:T(8,128)S(1)} %multiply_add_fusion, pred[]{:T(512)S(6)} %eq.176, f32[24,128,128]{2,1,0:T(8,128)S(1)} %bitcast.118, f32[24,128,128]{2,1,0:T(8,128)S(1)} %copy-done.21), kind=kOutput, calls=%fused_computation.54 | convolution fusion | flops 605552640 | bytes 7864321 | tf_op jit(solution)/shard_map/bij,bkj->bik/dot_general | solution.py:882
  297.5 28.5 %renew.1 = f32[24,128,128]{2,1,0:T(8,128)} custom-call(f32[24,128,128]{2,1,0:T(8,128)} %get-tuple-element.93.stat_ref, f32[24,128,128]{2,1,0:T(8,128)} %broadcast_select_fusion.2.basis_ref), custom_call_target="tpu_custom_call" | custom-call | tf_op jit(solution)/shard_map/renew/pallas_call | solution.py:871
  329.1 4.6 %multiply_subtract_fusion.1 = (f32[513,529]{1,0:T(8,128)S(1)}, f32[513,529]{1,0:T(8,128)}, f32[513,529]{1,0:T(8,128)}) fusion(f32[513,529]{1,0:T(8,128)S(1)} %copy-done.11, f32[]{:T(128)S(6)} %div.195, f32[1,640]{1,0:T(1,128)S(1)} %constant_dynamic-update-slice_fusion.13, f32[512,640]{1,0:T(8,128)S(1)} %copy-done.2, f32[513,255]{1,0:T(8,128)S(1)} %get-tuple-element.59, ...), kind=kLoop, calls=%fused_computation.39 | loop fusion | flops 5970294 | bytes 8872852 | tf_op jit(solution)/shard_map/sub | solution.py:922
  335.6 1.4 multiply_subtract_fusion.2
  338.1 2.1 multiply_add_fusion.2
  340.3 2.5 fusion.3
  342.9 4.5 %multiply_subtract_fusion = f32[24,128,128]{2,1,0:T(8,128)} fusion(f32[24,128,128]{2,1,0:T(8,128)S(1)} %copy-done.20, f32[24,128,128]{1,2,0:T(8,128)S(1)} %fusion.3, f32[24,128,128]{2,1,0:T(8,128)S(1)} %copy-done.1), kind=kOutput, calls=%fused_computation.21 | convolution fusion | flops 605552640 | bytes 6291456 | tf_op jit(solution)/shard_map/bij,bkj->bik/dot_general | solution.py:898
  347.4 3.4 broadcast_select_fusion
  (297 shorter events, 47.5 us)
Async XLA Ops:
  0.7 8.4 %copy-start.43 = (s32[192]{0:T(256)S(1)}, s32[192]{0:T(256)}, u32[]{:S(2)}) copy-start(s32[192]{0:T(256)} %refs_0_.1) | copy-start | bytes 2308
  0.7 8.6 %copy-start.10 = (f32[513,529]{1,0:T(8,128)S(1)}, f32[513,529]{1,0:T(8,128)}, u32[]{:S(2)}) copy-start(f32[513,529]{1,0:T(8,128)} %param.45) | copy-start | bytes 3256528
  0.7 8.7 %copy-start.39 = (s32[8,64]{1,0:T(8,128)S(1)}, s32[8,64]{1,0:T(8,128)}, u32[]{:S(2)}) copy-start(s32[8,64]{1,0:T(8,128)} %param.27) | copy-start | bytes 6148
  0.7 11.6 %copy-start.27 = (s32[8,64,32]{1,2,0:T(8,128)S(1)}, s32[8,64,32]{1,2,0:T(8,128)}, u32[]{:S(2)}) copy-start(s32[8,64,32]{1,2,0:T(8,128)} %param.26) | copy-start | bytes 196612
  0.7 11.7 %copy-start.40 = (s32[8,64]{1,0:T(8,128)S(1)}, s32[8,64]{1,0:T(8,128)}, u32[]{:S(2)}) copy-start(s32[8,64]{1,0:T(8,128)} %param.30) | copy-start | bytes 6148
  1.9 12.0 %copy-start.46 = (s32[26,18]{0,1:T(8,128)S(1)}, s32[26,18]{0,1:T(8,128)}, u32[]{:S(2)}) copy-start(s32[26,18]{0,1:T(8,128)} %param.29) | copy-start | bytes 5620
  1.9 12.0 %copy-start.47 = (s32[8]{0:T(128)S(1)}, s32[8]{0:T(128)}, u32[]{:S(2)}) copy-start(s32[8]{0:T(128)} %param.28) | copy-start | bytes 100
  1.9 12.3 %copy-start.45 = (pred[8]{0:T(512)(128)(4,1)S(1)}, pred[8]{0:T(512)(128)(4,1)}, u32[]{:S(2)}) copy-start(pred[8]{0:T(512)(128)(4,1)} %constant.259.clone.1) | copy-start | bytes 28
  2.9 14.4 %collective-permute-start.12 = (bf16[1,320,128]{2,1,0:T(8,128)(2,1)S(1)}, bf16[1,320,128]{2,1,0:T(8,128)(2,1)S(1)}, u32[]{:S(2)}, u32[]{:S(2)}) collective-permute-start(bf16[1,320,128]{2,1,0:T(8,128)(2,1)S(1)} %maximum_bitcast_fusion.2), channel_id=1, source_target_pairs={{0,4},{1,5},{2,6},{3,7},{4,0},{5,1},{6,2},{7,3},{8,12},{9,13},{10,... | collective-permute-start | bytes 245768 | tf_op jit(solution)/shard_map/ppermute | solution.py:61
  7.0 11.9 %collective-permute-start.6 = (bf16[1,320,128]{2,1,0:T(8,128)(2,1)S(1)}, bf16[1,320,128]{2,1,0:T(8,128)(2,1)S(1)}, u32[]{:S(2)}, u32[]{:S(2)}) collective-permute-start(bf16[1,320,128]{2,1,0:T(8,128)(2,1)S(1)} %maximum_bitcast_fusion.1), channel_id=1, source_target_pairs={{0,16},{8,24},{16,0},{24,8},{1,17},{9,25},{17,1},{25,9},{2,18},{10... | collective-permute-start | bytes 245768 | tf_op jit(solution)/shard_map/ppermute | solution.py:61
  8.5 7.1 %collective-permute-start = (bf16[1,384,128]{2,1,0:T(8,128)(2,1)S(1)}, bf16[1,384,128]{2,1,0:T(8,128)(2,1)S(1)}, u32[]{:S(2)}, u32[]{:S(2)}) collective-permute-start(bf16[1,384,128]{2,1,0:T(8,128)(2,1)S(1)} %maximum_bitcast_fusion), channel_id=1, source_target_pairs={{0,4},{1,5},{2,6},{3,7},{4,0},{5,1},{6,2},{7,3},{8,12},{9,13},{10,... | collective-permute-start | bytes 294920 | tf_op jit(solution)/shard_map/ppermute | solution.py:61
  10.0 12.7 %copy-start = (s32[96]{0:T(128)}, s32[96]{0:T(128)S(1)}, u32[]{:S(2)}) copy-start(s32[96]{0:T(128)S(1)} %add.760.refs_3_) | copy-start | bytes 1156
  15.7 7.0 %collective-permute-start.1 = (bf16[2,384,128]{2,1,0:T(8,128)(2,1)S(1)}, bf16[2,384,128]{2,1,0:T(8,128)(2,1)S(1)}, u32[]{:S(2)}, u32[]{:S(2)}) collective-permute-start(bf16[2,384,128]{2,1,0:T(8,128)(2,1)S(1)} %pad_maximum_fusion.10), channel_id=1, source_target_pairs={{0,2},{1,3},{2,0},{3,1},{4,6},{5,7},{6,4},{7,5},{8,10},{9,11},{10,... | collective-permute-start | bytes 589832 | tf_op jit(solution)/shard_map/ppermute | solution.py:61
  17.3 8.6 %collective-permute-start.13 = (bf16[2,320,128]{2,1,0:T(8,128)(2,1)S(1)}, bf16[2,320,128]{2,1,0:T(8,128)(2,1)S(1)}, u32[]{:S(2)}, u32[]{:S(2)}) collective-permute-start(bf16[2,320,128]{2,1,0:T(8,128)(2,1)S(1)} %pad_maximum_fusion.12), channel_id=1, source_target_pairs={{0,1},{1,0},{2,3},{3,2},{4,5},{5,4},{6,7},{7,6},{8,9},{9,8},{10,11... | collective-permute-start | bytes 491528 | tf_op jit(solution)/shard_map/ppermute | solution.py:61
  18.9 9.9 %collective-permute-start.7 = (bf16[2,320,128]{2,1,0:T(8,128)(2,1)S(1)}, bf16[2,320,128]{2,1,0:T(8,128)(2,1)S(1)}, u32[]{:S(2)}, u32[]{:S(2)}) collective-permute-start(bf16[2,320,128]{2,1,0:T(8,128)(2,1)S(1)} %pad_maximum_fusion.11), channel_id=1, source_target_pairs={{0,4},{1,5},{2,6},{3,7},{4,0},{5,1},{6,2},{7,3},{8,12},{9,13},{10,... | collective-permute-start | bytes 491528 | tf_op jit(solution)/shard_map/ppermute | solution.py:61
  22.7 8.8 %collective-permute-start.2 = (bf16[4,384,128]{2,1,0:T(8,128)(2,1)S(1)}, bf16[4,384,128]{2,1,0:T(8,128)(2,1)S(1)}, u32[]{:S(2)}, u32[]{:S(2)}) collective-permute-start(bf16[4,384,128]{2,1,0:T(8,128)(2,1)S(1)} %pad_maximum_fusion.6), channel_id=1, source_target_pairs={{0,1},{1,0},{2,3},{3,2},{4,5},{5,4},{6,7},{7,6},{8,9},{9,8},{10,11... | collective-permute-start | bytes 1179656 | tf_op jit(solution)/shard_map/ppermute | solution.py:61
  25.9 11.5 %collective-permute-start.14 = (bf16[4,320,128]{2,1,0:T(8,128)(2,1)S(1)}, bf16[4,320,128]{2,1,0:T(8,128)(2,1)S(1)}, u32[]{:S(2)}, u32[]{:S(2)}) collective-permute-start(bf16[4,320,128]{2,1,0:T(8,128)(2,1)S(1)} %pad_maximum_fusion.8), channel_id=1, source_target_pairs={{0,16},{8,24},{16,0},{24,8},{1,17},{9,25},{17,1},{25,9},{2,18},{10... | collective-permute-start | bytes 983048 | tf_op jit(solution)/shard_map/ppermute | solution.py:61
  28.9 10.7 %collective-permute-start.8 = (bf16[4,320,128]{2,1,0:T(8,128)(2,1)S(1)}, bf16[4,320,128]{2,1,0:T(8,128)(2,1)S(1)}, u32[]{:S(2)}, u32[]{:S(2)}) collective-permute-start(bf16[4,320,128]{2,1,0:T(8,128)(2,1)S(1)} %pad_maximum_fusion.7), channel_id=1, source_target_pairs={{0,2},{1,3},{2,0},{3,1},{4,6},{5,7},{6,4},{7,5},{8,10},{9,11},{10,... | collective-permute-start | bytes 983048 | tf_op jit(solution)/shard_map/ppermute | solution.py:61
  31.6 10.2 %copy-start.12 = (bf16[8,384,128]{2,1,0:T(8,128)(2,1)}, bf16[8,384,128]{2,1,0:T(8,128)(2,1)S(1)}, u32[]{:S(2)}) copy-start(bf16[8,384,128]{2,1,0:T(8,128)(2,1)S(1)} %pad_maximum_fusion.2.refs_4_) | copy-start | bytes 2359300
  31.6 19.0 %collective-permute-start.3 = (bf16[8,384,128]{2,1,0:T(8,128)(2,1)S(1)}, bf16[8,384,128]{2,1,0:T(8,128)(2,1)}, u32[]{:S(2)}, u32[]{:S(2)}) collective-permute-start(bf16[8,384,128]{2,1,0:T(8,128)(2,1)S(1)} %pad_maximum_fusion.2.refs_4_), channel_id=1, source_target_pairs={{0,16},{8,24},{16,0},{24,8},{1,17},{9,25},{17,1},{25,9},{2,18},{10... | collective-permute-start | bytes 2359304 | tf_op jit(solution)/shard_map/ppermute | solution.py:61
  37.5 18.4 %copy-start.15 = (bf16[8,320,128]{2,1,0:T(8,128)(2,1)}, bf16[8,320,128]{2,1,0:T(8,128)(2,1)S(1)}, u32[]{:S(2)}) copy-start(bf16[8,320,128]{2,1,0:T(8,128)(2,1)S(1)} %pad_maximum_fusion.4.refs_12_) | copy-start | bytes 1966084
  37.5 19.3 %copy-start.33 = (s32[8,64,32]{1,2,0:T(8,128)S(1)}, s32[8,64,32]{1,2,0:T(8,128)}, u32[]{:S(2)}) copy-start(s32[8,64,32]{1,2,0:T(8,128)} %pad_add_fusion) | copy-start | bytes 196612
  37.5 13.2 %collective-permute-start.15 = (bf16[8,320,128]{2,1,0:T(8,128)(2,1)S(1)}, bf16[8,320,128]{2,1,0:T(8,128)(2,1)}, u32[]{:S(2)}, u32[]{:S(2)}) collective-permute-start(bf16[8,320,128]{2,1,0:T(8,128)(2,1)S(1)} %pad_maximum_fusion.4.refs_12_), channel_id=1, source_target_pairs={{0,2},{1,3},{2,0},{3,1},{4,6},{5,7},{6,4},{7,5},{8,10},{9,11},{10,... | collective-permute-start | bytes 1966088 | tf_op jit(solution)/shard_map/ppermute | solution.py:61
  37.6 13.7 %collective-permute-start.16 = (bf16[8,320,128]{2,1,0:T(8,128)(2,1)S(1)}, bf16[8,320,128]{2,1,0:T(8,128)(2,1)S(1)}, u32[]{:S(2)}, u32[]{:S(2)}) collective-permute-start(bf16[8,320,128]{2,1,0:T(8,128)(2,1)S(1)} %pad_maximum_fusion.4.refs_12_), channel_id=1, source_target_pairs={{0,8},{8,0},{16,24},{24,16},{1,9},{9,1},{17,25},{25,17},{2,10},{10... | collective-permute-start | bytes 1966088 | tf_op jit(solution)/shard_map/ppermute | solution.py:61
  39.6 18.0 %copy-start.16 = (bf16[8,320,128]{2,1,0:T(8,128)(2,1)}, bf16[8,320,128]{2,1,0:T(8,128)(2,1)S(1)}, u32[]{:S(2)}) copy-start(bf16[8,320,128]{2,1,0:T(8,128)(2,1)S(1)} %pad_maximum_fusion.3.refs_8_) | copy-start | bytes 1966084
  39.6 17.6 %copy-start.42 = (s32[8,64,2]{1,2,0:T(2,128)S(1)}, s32[8,64,2]{1,2,0:T(2,128)}, u32[]{:S(2)}) copy-start(s32[8,64,2]{1,2,0:T(2,128)} %param.31) | copy-start | bytes 12292
  39.6 15.4 %collective-permute-start.9 = (bf16[8,320,128]{2,1,0:T(8,128)(2,1)S(1)}, bf16[8,320,128]{2,1,0:T(8,128)(2,1)}, u32[]{:S(2)}, u32[]{:S(2)}) collective-permute-start(bf16[8,320,128]{2,1,0:T(8,128)(2,1)S(1)} %pad_maximum_fusion.3.refs_8_), channel_id=1, source_target_pairs={{0,1},{1,0},{2,3},{3,2},{4,5},{5,4},{6,7},{7,6},{8,9},{9,8},{10,11... | collective-permute-start | bytes 1966088 | tf_op jit(solution)/shard_map/ppermute | solution.py:61
  40.9 16.6 %copy-start.44 = (s32[8,64]{1,0:T(8,128)S(1)}, s32[8,64]{1,0:T(8,128)}, u32[]{:S(2)}) copy-start(s32[8,64]{1,0:T(8,128)} %param.33) | copy-start | bytes 6148
  40.9 16.9 %copy-start.41 = (f32[8,64,2]{1,2,0:T(2,128)S(1)}, f32[8,64,2]{1,2,0:T(2,128)}, u32[]{:S(2)}) copy-start(f32[8,64,2]{1,2,0:T(2,128)} %param.32) | copy-start | bytes 12292
  41.8 24.6 %collective-permute-start.4 = (bf16[8,384,128]{2,1,0:T(8,128)(2,1)S(1)}, bf16[8,384,128]{2,1,0:T(8,128)(2,1)}, u32[]{:S(2)}, u32[]{:S(2)}) collective-permute-start(bf16[8,384,128]{2,1,0:T(8,128)(2,1)S(1)} %pad_maximum_fusion.2.refs_4_), channel_id=1, source_target_pairs={{0,8},{8,0},{16,24},{24,16},{1,9},{9,1},{17,25},{25,17},{2,10},{10... | collective-permute-start | bytes 2359304 | tf_op jit(solution)/shard_map/ppermute | solution.py:61
  50.7 15.8 %collective-permute-start.5 = (bf16[8,384,128]{2,1,0:T(8,128)(2,1)}, bf16[8,384,128]{2,1,0:T(8,128)(2,1)}, u32[]{:S(2)}, u32[]{:S(2)}) collective-permute-start(bf16[8,384,128]{2,1,0:T(8,128)(2,1)} %collective-permute-done.3.refs_5_), channel_id=1, source_target_pairs={{0,8},{8,0},{16,24},{24,16},{1,9},{9,1},{17,25},{25,17},{2,10},{10... | collective-permute-start | bytes 2359304 | tf_op jit(solution)/shard_map/ppermute | solution.py:61
  50.7 15.8 %collective-permute-start.10 = (bf16[8,320,128]{2,1,0:T(8,128)(2,1)S(1)}, bf16[8,320,128]{2,1,0:T(8,128)(2,1)}, u32[]{:S(2)}, u32[]{:S(2)}) collective-permute-start(bf16[8,320,128]{2,1,0:T(8,128)(2,1)S(1)} %pad_maximum_fusion.3.refs_8_), channel_id=1, source_target_pairs={{0,8},{8,0},{16,24},{24,16},{1,9},{9,1},{17,25},{25,17},{2,10},{10... | collective-permute-start | bytes 1966088 | tf_op jit(solution)/shard_map/ppermute | solution.py:61
  51.3 15.2 %collective-permute-start.17 = (bf16[8,320,128]{2,1,0:T(8,128)(2,1)}, bf16[8,320,128]{2,1,0:T(8,128)(2,1)}, u32[]{:S(2)}, u32[]{:S(2)}) collective-permute-start(bf16[8,320,128]{2,1,0:T(8,128)(2,1)} %collective-permute-done.15.refs_13_), channel_id=1, source_target_pairs={{0,8},{8,0},{16,24},{24,16},{1,9},{9,1},{17,25},{25,17},{2,10},{10... | collective-permute-start | bytes 1966088 | tf_op jit(solution)/shard_map/ppermute | solution.py:61
  55.1 11.4 %collective-permute-start.11 = (bf16[8,320,128]{2,1,0:T(8,128)(2,1)}, bf16[8,320,128]{2,1,0:T(8,128)(2,1)}, u32[]{:S(2)}, u32[]{:S(2)}) collective-permute-start(bf16[8,320,128]{2,1,0:T(8,128)(2,1)} %collective-permute-done.9.refs_9_), channel_id=1, source_target_pairs={{0,8},{8,0},{16,24},{24,16},{1,9},{9,1},{17,25},{25,17},{2,10},{10... | collective-permute-start | bytes 1966088 | tf_op jit(solution)/shard_map/ppermute | solution.py:61
  150.6 3.7 %collective-permute-start.23 = (bf16[16,368,128]{2,1,0:T(8,128)(2,1)}, bf16[16,368,128]{2,1,0:T(8,128)(2,1)S(1)}, u32[]{:S(2)}, u32[]{:S(2)}) collective-permute-start(bf16[16,368,128]{2,1,0:T(8,128)(2,1)} %get-tuple-element.29), channel_id=1, source_target_pairs={{0,8},{8,0},{16,24},{24,16},{1,9},{9,1},{17,25},{25,17},{2,10},{10... | collective-permute-start | bytes 4521992 | tf_op jit(solution)/shard_map/ppermute | solution.py:61
  151.2 7.6 %collective-permute-start.18 = (bf16[16,368,128]{2,1,0:T(8,128)(2,1)}, bf16[16,368,128]{2,1,0:T(8,128)(2,1)S(1)}, u32[]{:S(2)}, u32[]{:S(2)}) collective-permute-start(bf16[16,368,128]{2,1,0:T(8,128)(2,1)} %get-tuple-element.27), channel_id=1, source_target_pairs={{0,8},{8,0},{16,24},{24,16},{1,9},{9,1},{17,25},{25,17},{2,10},{10... | collective-permute-start | bytes 4521992 | tf_op jit(solution)/shard_map/ppermute | solution.py:61
  151.3 8.2 %collective-permute-start.28 = (bf16[16,384,128]{2,1,0:T(8,128)(2,1)}, bf16[16,384,128]{2,1,0:T(8,128)(2,1)S(1)}, u32[]{:S(2)}, u32[]{:S(2)}) collective-permute-start(bf16[16,384,128]{2,1,0:T(8,128)(2,1)} %get-tuple-element.32), channel_id=1, source_target_pairs={{0,8},{8,0},{16,24},{24,16},{1,9},{9,1},{17,25},{25,17},{2,10},{10... | collective-permute-start | bytes 4718600 | tf_op jit(solution)/shard_map/ppermute | solution.py:61
  156.8 19.4 %collective-permute-start.24 = (bf16[8,368,128]{2,1,0:T(8,128)(2,1)S(1)}, bf16[8,368,128]{2,1,0:T(8,128)(2,1)S(1)}, u32[]{:S(2)}, u32[]{:S(2)}) collective-permute-start(bf16[8,368,128]{2,1,0:T(8,128)(2,1)S(1)} %slice.541), channel_id=1, source_target_pairs={{0,2},{1,3},{2,0},{3,1},{4,6},{5,7},{6,4},{7,5},{8,10},{9,11},{10,... | collective-permute-start | bytes 2261000 | tf_op jit(solution)/shard_map/ppermute | solution.py:61
  159.1 19.3 %collective-permute-start.19 = (bf16[8,368,128]{2,1,0:T(8,128)(2,1)S(1)}, bf16[8,368,128]{2,1,0:T(8,128)(2,1)S(1)}, u32[]{:S(2)}, u32[]{:S(2)}) collective-permute-start(bf16[8,368,128]{2,1,0:T(8,128)(2,1)S(1)} %slice.542), channel_id=1, source_target_pairs={{0,1},{1,0},{2,3},{3,2},{4,5},{5,4},{6,7},{7,6},{8,9},{9,8},{10,11... | collective-permute-start | bytes 2261000 | tf_op jit(solution)/shard_map/ppermute | solution.py:61
  161.1 20.5 %collective-permute-start.29 = (bf16[8,384,128]{2,1,0:T(8,128)(2,1)S(1)}, bf16[8,384,128]{2,1,0:T(8,128)(2,1)S(1)}, u32[]{:S(2)}, u32[]{:S(2)}) collective-permute-start(bf16[8,384,128]{2,1,0:T(8,128)(2,1)S(1)} %slice.540), channel_id=1, source_target_pairs={{0,16},{8,24},{16,0},{24,8},{1,17},{9,25},{17,1},{25,9},{2,18},{10... | collective-permute-start | bytes 2359304 | tf_op jit(solution)/shard_map/ppermute | solution.py:61
  176.3 12.8 %collective-permute-start.25 = (bf16[4,368,128]{2,1,0:T(8,128)(2,1)S(1)}, bf16[4,368,128]{2,1,0:T(8,128)(2,1)S(1)}, u32[]{:S(2)}, u32[]{:S(2)}) collective-permute-start(bf16[4,368,128]{2,1,0:T(8,128)(2,1)S(1)} %slice.544), channel_id=1, source_target_pairs={{0,16},{8,24},{16,0},{24,8},{1,17},{9,25},{17,1},{25,9},{2,18},{10... | collective-permute-start | bytes 1130504 | tf_op jit(solution)/shard_map/ppermute | solution.py:61
  178.7 11.0 %collective-permute-start.20 = (bf16[4,368,128]{2,1,0:T(8,128)(2,1)S(1)}, bf16[4,368,128]{2,1,0:T(8,128)(2,1)S(1)}, u32[]{:S(2)}, u32[]{:S(2)}) collective-permute-start(bf16[4,368,128]{2,1,0:T(8,128)(2,1)S(1)} %slice.545), channel_id=1, source_target_pairs={{0,2},{1,3},{2,0},{3,1},{4,6},{5,7},{6,4},{7,5},{8,10},{9,11},{10,... | collective-permute-start | bytes 1130504 | tf_op jit(solution)/shard_map/ppermute | solution.py:61
  181.9 10.5 %collective-permute-start.30 = (bf16[4,384,128]{2,1,0:T(8,128)(2,1)S(1)}, bf16[4,384,128]{2,1,0:T(8,128)(2,1)S(1)}, u32[]{:S(2)}, u32[]{:S(2)}) collective-permute-start(bf16[4,384,128]{2,1,0:T(8,128)(2,1)S(1)} %slice.543), channel_id=1, source_target_pairs={{0,1},{1,0},{2,3},{3,2},{4,5},{5,4},{6,7},{7,6},{8,9},{9,8},{10,11... | collective-permute-start | bytes 1179656 | tf_op jit(solution)/shard_map/ppermute | solution.py:61
  189.2 6.7 %collective-permute-start.26 = (bf16[2,368,128]{2,1,0:T(8,128)(2,1)S(1)}, bf16[2,368,128]{2,1,0:T(8,128)(2,1)S(1)}, u32[]{:S(2)}, u32[]{:S(2)}) collective-permute-start(bf16[2,368,128]{2,1,0:T(8,128)(2,1)S(1)} %slice.547), channel_id=1, source_target_pairs={{0,1},{1,0},{2,3},{3,2},{4,5},{5,4},{6,7},{7,6},{8,9},{9,8},{10,11... | collective-permute-start | bytes 565256 | tf_op jit(solution)/shard_map/ppermute | solution.py:61
  189.7 12.9 %collective-permute-start.21 = (bf16[2,368,128]{2,1,0:T(8,128)(2,1)S(1)}, bf16[2,368,128]{2,1,0:T(8,128)(2,1)S(1)}, u32[]{:S(2)}, u32[]{:S(2)}) collective-permute-start(bf16[2,368,128]{2,1,0:T(8,128)(2,1)S(1)} %slice.548), channel_id=1, source_target_pairs={{0,4},{1,5},{2,6},{3,7},{4,0},{5,1},{6,2},{7,3},{8,12},{9,13},{10,... | collective-permute-start | bytes 565256 | tf_op jit(solution)/shard_map/ppermute | solution.py:61
  192.5 11.6 %collective-permute-start.31 = (bf16[2,384,128]{2,1,0:T(8,128)(2,1)S(1)}, bf16[2,384,128]{2,1,0:T(8,128)(2,1)S(1)}, u32[]{:S(2)}, u32[]{:S(2)}) collective-permute-start(bf16[2,384,128]{2,1,0:T(8,128)(2,1)S(1)} %slice.546), channel_id=1, source_target_pairs={{0,2},{1,3},{2,0},{3,1},{4,6},{5,7},{6,4},{7,5},{8,10},{9,11},{10,... | collective-permute-start | bytes 589832 | tf_op jit(solution)/shard_map/ppermute | solution.py:61
  196.0 17.3 %collective-permute-start.27 = (f32[1,368,128]{2,1,0:T(8,128)S(1)}, f32[1,368,128]{2,1,0:T(8,128)S(1)}, u32[]{:S(2)}, u32[]{:S(2)}) collective-permute-start(f32[1,368,128]{2,1,0:T(8,128)S(1)} %slice.421), channel_id=1, source_target_pairs={{0,4},{1,5},{2,6},{3,7},{4,0},{5,1},{6,2},{7,3},{8,12},{9,13},{10,... | collective-permute-start | bytes 565256 | tf_op jit(solution)/shard_map/ppermute | solution.py:61
  202.7 11.3 %collective-permute-start.22 = (f32[1,368,128]{2,1,0:T(8,128)S(1)}, f32[1,368,128]{2,1,0:T(8,128)S(1)}, u32[]{:S(2)}, u32[]{:S(2)}) collective-permute-start(f32[1,368,128]{2,1,0:T(8,128)S(1)} %slice.412), channel_id=1, source_target_pairs={{0,16},{8,24},{16,0},{24,8},{1,17},{9,25},{17,1},{25,9},{2,18},{10... | collective-permute-start | bytes 565256 | tf_op jit(solution)/shard_map/ppermute | solution.py:61
  204.2 12.9 %collective-permute-start.32 = (f32[1,384,128]{2,1,0:T(8,128)S(1)}, f32[1,384,128]{2,1,0:T(8,128)S(1)}, u32[]{:S(2)}, u32[]{:S(2)}) collective-permute-start(f32[1,384,128]{2,1,0:T(8,128)S(1)} %slice.430), channel_id=1, source_target_pairs={{0,4},{1,5},{2,6},{3,7},{4,0},{5,1},{6,2},{7,3},{8,12},{9,13},{10,... | collective-permute-start | bytes 589832 | tf_op jit(solution)/shard_map/ppermute | solution.py:61
  219.8 4.2 %collective-permute-start.33 = (f32[1,104,128]{2,1,0:T(8,128)S(1)}, f32[1,104,128]{2,1,0:T(8,128)S(1)}, u32[]{:S(2)}, u32[]{:S(2)}) collective-permute-start(f32[1,104,128]{2,1,0:T(8,128)S(1)} %fusion.26), channel_id=1, source_target_pairs={{0,16},{8,24},{16,0},{24,8},{1,17},{9,25},{17,1},{25,9},{2,18},{10... | collective-permute-start | bytes 159752 | tf_op jit(solution)/shard_map/ppermute | solution.py:61
  223.9 4.8 %collective-permute-start.34 = (f32[2,104,128]{2,1,0:T(8,128)S(1)}, f32[2,104,128]{2,1,0:T(8,128)S(1)}, u32[]{:S(2)}, u32[]{:S(2)}) collective-permute-start(f32[2,104,128]{2,1,0:T(8,128)S(1)} %pad_maximum_fusion.13), channel_id=1, source_target_pairs={{0,2},{1,3},{2,0},{3,1},{4,6},{5,7},{6,4},{7,5},{8,10},{9,11},{10,... | collective-permute-start | bytes 319496 | tf_op jit(solution)/shard_map/ppermute | solution.py:61
  228.7 5.9 %collective-permute-start.35 = (f32[4,104,128]{2,1,0:T(8,128)S(1)}, f32[4,104,128]{2,1,0:T(8,128)S(1)}, u32[]{:S(2)}, u32[]{:S(2)}) collective-permute-start(f32[4,104,128]{2,1,0:T(8,128)S(1)} %pad_maximum_fusion.9), channel_id=1, source_target_pairs={{0,1},{1,0},{2,3},{3,2},{4,5},{5,4},{6,7},{7,6},{8,9},{9,8},{10,11... | collective-permute-start | bytes 638984 | tf_op jit(solution)/shard_map/ppermute | solution.py:61
  231.2 12.1 %collective-permute-start.38 = (f32[1,1024,128]{2,1,0:T(8,128)}, f32[1,1024,128]{2,1,0:T(8,128)}, u32[]{:S(2)}, u32[]{:S(2)}) collective-permute-start(f32[1,1024,128]{2,1,0:T(8,128)} %bitcast.38), channel_id=1, source_target_pairs={{0,16},{8,24},{16,0},{24,8},{1,17},{9,25},{17,1},{25,9},{2,18},{10... | collective-permute-start | bytes 1572872 | tf_op jit(solution)/shard_map/ppermute | solution.py:61
  234.7 18.7 %collective-permute-start.36 = (f32[8,104,128]{2,1,0:T(8,128)S(1)}, f32[8,104,128]{2,1,0:T(8,128)S(1)}, u32[]{:S(2)}, u32[]{:S(2)}) collective-permute-start(f32[8,104,128]{2,1,0:T(8,128)S(1)} %pad_maximum_fusion.5), channel_id=1, source_target_pairs={{0,4},{1,5},{2,6},{3,7},{4,0},{5,1},{6,2},{7,3},{8,12},{9,13},{10,... | collective-permute-start | bytes 1277960 | tf_op jit(solution)/shard_map/ppermute | solution.py:61
  237.6 16.8 %copy-start.1 = (f32[24,128,128]{2,1,0:T(8,128)S(1)}, f32[24,128,128]{2,1,0:T(8,128)}, u32[]{:S(2)}) copy-start(f32[24,128,128]{2,1,0:T(8,128)} %param.41) | copy-start | bytes 4718596
  237.6 16.8 %copy-start.3 = (f32[24,128,128]{2,1,0:T(8,128)S(1)}, f32[24,128,128]{2,1,0:T(8,128)}, u32[]{:S(2)}) copy-start(f32[24,128,128]{2,1,0:T(8,128)} %param.40) | copy-start | bytes 4718596
  245.5 10.2 %collective-permute-start.39 = (f32[2,1024,128]{2,1,0:T(8,128)}, f32[2,1024,128]{2,1,0:T(8,128)}, u32[]{:S(2)}, u32[]{:S(2)}) collective-permute-start(f32[2,1024,128]{2,1,0:T(8,128)} %pad_maximum_fusion.1), channel_id=1, source_target_pairs={{0,8},{8,0},{16,24},{24,16},{1,9},{9,1},{17,25},{25,17},{2,10},{10... | collective-permute-start | bytes 3145736 | tf_op jit(solution)/shard_map/ppermute | solution.py:61
  254.3 8.0 %collective-permute-start.37 = (f32[16,104,128]{2,1,0:T(8,128)}, f32[16,104,128]{2,1,0:T(8,128)}, u32[]{:S(2)}, u32[]{:S(2)}) collective-permute-start(f32[16,104,128]{2,1,0:T(8,128)} %get-tuple-element.62), channel_id=1, source_target_pairs={{0,8},{8,0},{16,24},{24,16},{1,9},{9,1},{17,25},{25,17},{2,10},{10... | collective-permute-start | bytes 2555912 | tf_op jit(solution)/shard_map/ppermute | solution.py:61
  274.7 9.6 %copy-start.19 = (f32[4,256,128]{2,1,0:T(8,128)S(1)}, f32[4,256,128]{2,1,0:T(8,128)}, u32[]{:S(2)}) copy-start(f32[4,256,128]{2,1,0:T(8,128)} %slice_multiply_fusion.2) | copy-start | bytes 1572868
  274.7 10.8 %copy-start.4 = (f32[24,128,128]{2,1,0:T(8,128)S(1)}, f32[24,128,128]{2,1,0:T(8,128)}, u32[]{:S(2)}) copy-start(f32[24,128,128]{2,1,0:T(8,128)} %param.40) | copy-start | bytes 4718596
  297.5 30.3 %copy-start.2 = (f32[512,640]{1,0:T(8,128)S(1)}, f32[512,640]{1,0:T(8,128)}, u32[]{:S(2)}) copy-start(f32[512,640]{1,0:T(8,128)} %slice_dynamic-update-slice_fusion) | copy-start | bytes 3932164
  326.0 21.4 %collective-permute-start.40 = (f32[24,128,128]{2,1,0:T(8,128)}, f32[24,128,128]{2,1,0:T(8,128)}, u32[]{:S(2)}, u32[]{:S(2)}) collective-permute-start(f32[24,128,128]{2,1,0:T(8,128)} %renew.1), channel_id=1, source_target_pairs={{0,8},{8,0},{16,24},{24,16},{1,9},{9,1},{17,25},{25,17},{2,10},{10... | collective-permute-start | bytes 4718600 | tf_op jit(solution)/shard_map/ppermute | solution.py:61
  329.1 6.4 %copy-start.31 = (f32[256,512]{1,0:T(8,128)S(1)}, f32[256,512]{1,0:T(8,128)}, u32[]{:S(2)}) copy-start(f32[256,512]{1,0:T(8,128)} %param.43) | copy-start | bytes 1572868
  329.1 6.4 %copy-start.32 = (f32[256,512]{1,0:T(8,128)S(1)}, f32[256,512]{1,0:T(8,128)}, u32[]{:S(2)}) copy-start(f32[256,512]{1,0:T(8,128)} %param.44) | copy-start | bytes 1572868
  (25 other events, 72.6 us)
